TPU v7x, 32 devices: a whole 2x2x4 slice. The times are simulated.
32 devices in a mesh: dp: 4 (over y, core), bucket: 8 (over z, x).
Axes of the slice: x: 2, y: 2, z: 4, core: 2. Of those that a mesh axis runs over, the one named last changes fastest.
Arguments:
- frames: bfloat16 [49152, 512], P(('dp', 'bucket')), may hold values from -60 to 60, as said below
- lengths: int32 [4, 256], P('dp'), may hold values from 1 to 48, as said below
- owners: int32 [4, 256], P('dp'), may hold values from 0 to 7, as said below
- upstream: bfloat16 [24576, 512], P(('dp', 'bucket')), may hold values from -6 to 6
- ln_gain: float32 [512], replicated, may hold values from 0.1 to 1.9
- w_in: bfloat16 [512, 1024], replicated, may hold values from -0.25 to 0.25
- w_dw: float32 [512, 31], replicated, may hold values from -1 to 1
- bn_gain: float32 [512], replicated, may hold values from 0.1 to 1.9
- bn_bias: float32 [512], replicated, may hold values from -3 to 3
- w_out: bfloat16 [512, 512], replicated, may hold values from -0.25 to 0.25
Outputs:
- out_frames: bfloat16 [24576, 512], P(('dp', 'bucket'))
- grad_frames: bfloat16 [49152, 512], P(('dp', 'bucket'))
- grad_w_in: float32 [512, 1024], P('bucket')
- grad_w_out: float32 [512, 512], P('bucket')
- grad_w_dw: float32 [512, 31], P('bucket')
- grad_ln_gain: float32 [512], P('bucket')
- grad_bn_gain: float32 [512], replicated
- grad_bn_bias: float32 [512], replicated
Inputs may be any that keep to these rules, and one draw needn't show every extreme that they name: `frames`: frame rows past an utterance's length are not read. In each group every owner receives exactly 4 utterances from each loader shard, their lengths sum to exactly 768 with one of exactly 48, and the lengths an owner receives do not fall with the loader index. `owners`: in each group and loader shard every owner index appears exactly 4 times.
All inputs are finite; a program needn't handle non-finite values.
Results may differ from a plain program's by a relative error of at most 0.013.
Values may be sent and summed in bfloat16 or wider, within the bound.
A program may use at most 128 MiB of HBM per device.

v0:
```python
import functools

import jax
import jax.numpy as jnp
from jax import lax
from jax.experimental import pallas as pl
from jax.experimental.pallas import tpu as pltpu
from jax.sharding import PartitionSpec as P

EPSILON = 1e-05
LANES = 128
SUB = 8
MESH = pl.DeviceIdType.MESH
VMEM_LIMIT = 24 << 20


def lane(c):
    return slice(c * LANES, (c + 1) * LANES)


def row_of(packed, first, blocks):
    return jnp.concatenate([packed[first + c : first + c + 1] for c in range(blocks)], axis=1)


def live_rows(lens_ref, first, count, span, width):
    position = lax.broadcasted_iota(jnp.int32, (span, width), 0)
    return [position < lens_ref[0, first + i] for i in range(count)]


def keep_live(values, masks, span):
    parts = [
        jnp.where(masks[i], values[i * span : (i + 1) * span], 0.0) for i in range(len(masks))
    ]
    return jnp.concatenate(parts, axis=0)


def layer_norm(frame_rows):
    values = frame_rows.astype(jnp.float32)
    centred = values - jnp.mean(values, axis=1, keepdims=True)
    inverse = lax.rsqrt(jnp.mean(centred * centred, axis=1, keepdims=True) + EPSILON)
    return centred * inverse, inverse


def project(frame_rows, gain, w_in):
    normed, inverse = layer_norm(frame_rows)
    h = (normed * gain).astype(jnp.bfloat16)
    projected = jnp.dot(h, w_in, preferred_element_type=jnp.float32)
    half = projected.shape[1] // 2
    return normed, inverse, projected[:, :half], jax.nn.sigmoid(projected[:, half:])


def shifted_sum(frame, weight, span, taps):
    lead = (taps + 1) // 2 // SUB
    count = span // SUB
    tiles = [frame[i * SUB : (i + 1) * SUB] for i in range(count)]
    total = None
    for residue in range(SUB):
        shifts = [k for k in range(residue, taps + 1, SUB) if k > 0]
        weights = {k: jnp.broadcast_to(weight(k), (SUB, LANES)) for k in shifts}
        parts = []
        for i in range(count + 1 if residue else count):
            part = None
            for k in shifts:
                at = (k - residue) // SUB + i - lead
                if 0 <= at < count:
                    term = tiles[at] * weights[k]
                    part = term if part is None else part + term
            parts.append(jnp.zeros((SUB, LANES), jnp.float32) if part is None else part)
        moved = jnp.concatenate(parts, axis=0)
        if residue:
            moved = pltpu.roll(moved, span + SUB - residue, 0)[:span]
        total = moved if total is None else total + moved
    return total


def forward_kernel(group, span, taps, lens_ref, frames_ref, gain_ref, w_in_ref, w_dw_ref,
                   conv_ref, sums_ref, normed_ref, inverse_ref, linear_ref, gate_ref, padded):
    step = pl.program_id(0)
    blocks = conv_ref.shape[1] // LANES

    @pl.when(step == 0)
    def _():
        sums_ref[...] = jnp.zeros_like(sums_ref)

    masks = live_rows(lens_ref, step * group, group, span, conv_ref.shape[1])
    normed, inverse, linear, gate = project(frames_ref[...], gain_ref[...], w_in_ref[...])
    normed_ref[...] = normed
    inverse_ref[...] = jnp.broadcast_to(inverse, inverse_ref.shape)
    linear_ref[...] = linear
    gate_ref[...] = gate
    gated = keep_live(linear * gate, masks, span).astype(jnp.bfloat16).astype(jnp.float32)
    for u in range(group):
        for c in range(blocks):
            padded[u, c] = gated[u * span : (u + 1) * span, lane(c)]

    def one(u, carry):
        live = lax.broadcasted_iota(jnp.int32, (span, LANES), 0) < lens_ref[0, step * group + u]
        start = pl.multiple_of(u * span, SUB)
        for c in range(blocks):
            conv = shifted_sum(
                padded[u, c], lambda k: w_dw_ref[k - 1 : k, lane(c)], span, taps
            )
            conv_ref[pl.ds(start, span), lane(c)] = conv
            masked = jnp.where(live, conv, 0.0)
            sums_ref[c : c + 1] += jnp.sum(masked, axis=0, keepdims=True)
            sums_ref[blocks + c : blocks + c + 1] += jnp.sum(
                masked * masked, axis=0, keepdims=True
            )
        return carry

    lax.fori_loop(0, group, one, 0)


def batch_norm(total_ref, conv, total_frames, blocks):
    packed = total_ref[...]
    centre = row_of(packed, 0, blocks) / total_frames
    variance = row_of(packed, blocks, blocks) / total_frames - centre * centre
    inverse = lax.rsqrt(variance + EPSILON)
    return (conv - centre) * inverse, inverse


def middle_kernel(group, span, total_frames, lens_ref, conv_ref, dy_ref, total_ref, bn_gain_ref,
                  bn_bias_ref, w_out_ref, out_ref, grad_bn_ref, sums_ref, grad_wout_ref):
    step = pl.program_id(0)
    width = conv_ref.shape[1]
    blocks = width // LANES

    @pl.when(step == 0)
    def _():
        sums_ref[...] = jnp.zeros_like(sums_ref)
        grad_wout_ref[...] = jnp.zeros_like(grad_wout_ref)

    masks = live_rows(lens_ref, step * group, group, span, width)
    slots = [lens_ref[1, step * group + i] for i in range(group)]
    arrived = jnp.concatenate([dy_ref[slot] for slot in slots], axis=0)
    dy = keep_live(arrived.astype(jnp.float32), masks, span).astype(jnp.bfloat16)
    w_out = w_out_ref[...]
    bn_normed, _ = batch_norm(total_ref, conv_ref[...], total_frames, blocks)
    bn = bn_normed * bn_gain_ref[...] + bn_bias_ref[...]
    sig = jax.nn.sigmoid(bn)
    swished = (bn * sig).astype(jnp.bfloat16)
    out = jnp.dot(swished, w_out, preferred_element_type=jnp.float32).astype(jnp.bfloat16)
    for i in range(group):
        out_ref[slots[i]] = out[i * span : (i + 1) * span]
    grad_wout_ref[...] += lax.dot_general(
        swished, dy, (((0,), (0,)), ((), ())), preferred_element_type=jnp.float32
    )
    grad_swish = lax.dot_general(
        dy, w_out, (((1,), (1,)), ((), ())), preferred_element_type=jnp.float32
    )
    grad_bn = grad_swish * (sig * (1.0 + bn * (1.0 - sig)))
    grad_bn_ref[...] = grad_bn
    bias_row = jnp.sum(grad_bn, axis=0, keepdims=True)
    gain_row = jnp.sum(grad_bn * bn_normed, axis=0, keepdims=True)
    for c in range(blocks):
        sums_ref[c : c + 1] += bias_row[:, lane(c)]
        sums_ref[blocks + c : blocks + c + 1] += gain_row[:, lane(c)]


def backward_kernel(group, span, taps, total_frames, lens_ref, normed_ref, inverse_ref,
                    linear_ref, gate_ref, conv_ref, grad_bn_ref,
                    total_ref, back_ref, gain_ref, bn_gain_ref, w_in_ref, w_dw_ref, wout_ref,
                    grad_frames_ref, packed_ref, padded, grad_pad, gated_grad, w_acc, win_acc,
                    ln_acc, flat):
    step = pl.program_id(0)
    width = conv_ref.shape[1]
    blocks = width // LANES
    count = span // SUB
    lead = (taps + 1) // 2 // SUB

    @pl.when(step == 0)
    def _():
        w_acc[...] = jnp.zeros_like(w_acc)
        win_acc[...] = jnp.zeros_like(win_acc)
        ln_acc[...] = jnp.zeros_like(ln_acc)

    masks = live_rows(lens_ref, step * group, group, span, width)
    w_in = w_in_ref[...]
    gated = keep_live(linear_ref[...] * gate_ref[...], masks, span).astype(jnp.bfloat16).astype(jnp.float32)
    bn_normed, bn_inverse = batch_norm(total_ref, conv_ref[...], total_frames, blocks)
    back = back_ref[...]
    bias_mean = row_of(back, 0, blocks) / total_frames
    gain_mean = row_of(back, blocks, blocks) / total_frames
    grad_conv = keep_live(
        bn_gain_ref[...] * bn_inverse * (grad_bn_ref[...] - bias_mean - bn_normed * gain_mean),
        masks,
        span,
    )
    for u in range(group):
        for c in range(blocks):
            rows = slice(u * span, (u + 1) * span)
            padded[u, c] = gated[rows, lane(c)]
            grad_pad[u, c] = grad_conv[rows, lane(c)]

    def one(u, carry):
        start = pl.multiple_of(u * span, SUB)
        for c in range(blocks):
            grads = grad_pad[u, c]
            gated_grad[pl.ds(start, span), lane(c)] = shifted_sum(
                grads, lambda k: w_dw_ref[taps - k : taps - k + 1, lane(c)], span, taps
            )
            blank = jnp.zeros((SUB, LANES), jnp.float32)
            inner = jnp.concatenate([blank, grads, blank], axis=0)
            frame = padded[u, c]
            for residue in range(SUB):
                moved = inner if residue == 0 else pltpu.roll(inner, residue, 0)
                moved = moved[SUB:]
                for k in range(residue, taps + 1, SUB):
                    if k == 0:
                        continue
                    part = None
                    for i in range(count + 1 if residue else count):
                        at = (k - residue) // SUB + i - lead
                        if 0 <= at < count:
                            tile = frame[at * SUB : (at + 1) * SUB]
                            term = moved[i * SUB : (i + 1) * SUB] * tile
                            part = term if part is None else part + term
                    w_acc[c, k - 1] += part
        return carry

    lax.fori_loop(0, group, one, 0)

    grad_gated = keep_live(gated_grad[...], masks, span)
    linear, gate = linear_ref[...], gate_ref[...]
    normed, inverse = normed_ref[...], inverse_ref[:, :1]
    h = (normed * gain_ref[...]).astype(jnp.bfloat16)
    left = grad_gated * gate
    grad_a = jnp.concatenate(
        [left.astype(jnp.bfloat16), (left * linear * (1.0 - gate)).astype(jnp.bfloat16)], axis=1
    )
    win_acc[...] += lax.dot_general(
        h, grad_a, (((0,), (0,)), ((), ())), preferred_element_type=jnp.float32
    )
    grad_h = lax.dot_general(
        grad_a, w_in, (((1,), (1,)), ((), ())), preferred_element_type=jnp.float32
    )
    ln_acc[...] += jnp.sum(grad_h * normed, axis=0, keepdims=True)
    scaled = grad_h * gain_ref[...]
    inner_mean = jnp.mean(scaled * normed, axis=1, keepdims=True)
    grad_x = inverse * (scaled - jnp.mean(scaled, axis=1, keepdims=True) - normed * inner_mean)
    grad_frames_ref[...] = keep_live(grad_x, masks, span).astype(jnp.bfloat16)

    @pl.when(step == pl.num_programs(0) - 1)
    def _():
        owners = packed_ref.shape[0]
        share = width // owners
        wide = w_in.shape[1] // LANES
        for c in range(blocks):
            flat[...] = jnp.zeros_like(flat)
            for k in range(taps):
                flat[k : k + 1] = jnp.sum(w_acc[c, k], axis=0, keepdims=True)
            flat[taps : taps + 1] = ln_acc[:, lane(c)]
            turned = flat[...].T.astype(jnp.bfloat16)
            for i in range(LANES // share):
                packed_ref[c * (LANES // share) + i, (wide + blocks) * share :] = turned[
                    i * share : (i + 1) * share
                ]
        for j in range(owners):
            rows = slice(j * share, (j + 1) * share)
            for c in range(wide):
                packed_ref[j, c * share : (c + 1) * share] = win_acc[rows, lane(c)].astype(
                    jnp.bfloat16
                )
            for c in range(blocks):
                packed_ref[j, (wide + c) * share : (wide + c + 1) * share] = wout_ref[
                    rows, lane(c)
                ].astype(jnp.bfloat16)


def plan_kernel(slots, lens_ref, owners_ref, up_ref, out_ref, meta_ref, stage, counts, begin):
    me = lax.axis_index("bucket")
    own_rows, width = up_ref.shape
    span = out_ref.shape[1]
    blocks = width // LANES
    loaders = lens_ref.shape[1] // slots
    pairs = slots // loaders
    for c in range(blocks):
        stage[c, :own_rows] = up_ref[:, lane(c)].astype(jnp.float32)
        stage[c, own_rows:] = jnp.zeros((span, LANES), jnp.float32)

    def look(i, carry):
        found, start = carry
        for j in range(SUB):
            at = i * SUB + j
            mine = owners_ref[0, at] == me
            begin[found] = start
            found = found + jnp.where(mine, 1, 0)
            start = start + jnp.where(mine, lens_ref[0, at], 0)
        return found, start

    lax.fori_loop(0, loaders * slots // SUB, look, (jnp.int32(0), jnp.int32(0)))

    def move(i, carry):
        start = begin[i]
        meta_ref[2, i] = start
        for c in range(blocks):
            out_ref[i, :, lane(c)] = stage[c, pl.ds(start, span)].astype(jnp.bfloat16)
        return carry

    lax.fori_loop(0, slots, move, 0)

    def clear(i, carry):
        counts[i] = 0
        return carry

    lax.fori_loop(0, loaders, clear, 0)

    def place(i, carry):
        owner = owners_ref[0, me * slots + i]
        rank = counts[owner]
        counts[owner] = rank + 1
        meta_ref[0, i] = lens_ref[0, me * slots + i]
        meta_ref[1, i] = owner * pairs + rank
        return carry

    lax.fori_loop(0, slots, place, 0)


def finish_kernel(meta_ref, arrived_ref, reduced_ref, out_ref, win_ref, wout_ref, last_ref, stage):
    slots, span, width = arrived_ref.shape
    own_rows = out_ref.shape[0]
    blocks = width // LANES
    wide = win_ref.shape[1] // LANES

    def place(u, carry):
        start = meta_ref[2, u]
        for c in range(blocks):
            stage[c, pl.ds(start, span)] = arrived_ref[u, :, lane(c)].astype(jnp.float32)
        return carry

    lax.fori_loop(0, slots, place, 0)
    for c in range(blocks):
        out_ref[:, lane(c)] = stage[c, :own_rows].astype(jnp.bfloat16)
        wout_ref[:, lane(c)] = reduced_ref[wide + c].astype(jnp.float32)
    for c in range(wide):
        win_ref[:, lane(c)] = reduced_ref[c].astype(jnp.float32)
    last_ref[...] = reduced_ref[wide + blocks].astype(jnp.float32)


def whole(shape):
    return pl.BlockSpec(shape, lambda i, *_: (0,) * len(shape))


def sum_kernel(groups, owners, part_ref, out_ref, slots, send_sems, recv_sems):
    count = groups * owners
    me = lax.axis_index("dp") * owners + lax.axis_index("bucket")
    barrier = pltpu.get_barrier_semaphore()

    def peer_of(i):
        other = lax.rem(me + i, count)
        return (other // owners, lax.rem(other, owners))

    def greet(i, carry):
        pl.semaphore_signal(barrier, inc=1, device_id=peer_of(i), device_id_type=MESH)
        return carry

    lax.fori_loop(1, count, greet, 0)
    pl.semaphore_wait(barrier, count - 1)

    def copy_to(i):
        return pltpu.make_async_remote_copy(
            src_ref=part_ref,
            dst_ref=slots.at[me],
            send_sem=send_sems.at[i],
            recv_sem=recv_sems.at[me],
            device_id=peer_of(i),
            device_id_type=MESH,
        )

    def send(i, carry):
        copy_to(i).start()
        return carry

    lax.fori_loop(1, count, send, 0)
    slots[me] = part_ref[...]

    def receive(i, carry):
        source = lax.rem(me + i, count)
        pltpu.make_async_remote_copy(
            src_ref=part_ref,
            dst_ref=slots.at[source],
            send_sem=send_sems.at[i],
            recv_sem=recv_sems.at[source],
            device_id=peer_of(i),
            device_id_type=MESH,
        ).wait_recv()
        return carry

    lax.fori_loop(1, count, receive, 0)
    out_ref[...] = lax.fori_loop(
        1, count, lambda i, total: total + slots[i], slots[0]
    )

    def sent(i, carry):
        copy_to(i).wait_send()
        return carry

    lax.fori_loop(1, count, sent, 0)


def sum_everywhere(part, collective_id):
    groups, owners = lax.axis_size("dp"), lax.axis_size("bucket")
    count = groups * owners
    return pl.pallas_call(
        functools.partial(sum_kernel, groups, owners),
        out_shape=jax.ShapeDtypeStruct(part.shape, part.dtype),
        in_specs=[pl.BlockSpec(memory_space=pltpu.VMEM)],
        out_specs=pl.BlockSpec(memory_space=pltpu.VMEM),
        scratch_shapes=[
            pltpu.VMEM((count,) + part.shape, part.dtype),
            pltpu.SemaphoreType.DMA((count,)),
            pltpu.SemaphoreType.DMA((count,)),
        ],
        compiler_params=pltpu.CompilerParams(
            collective_id=collective_id, has_side_effects=True, vmem_limit_bytes=4 << 20
        ),
        cost_estimate=pl.CostEstimate(flops=10**6, bytes_accessed=2 * 10**7, transcendentals=0),
        name="sum_everywhere_%d" % collective_id,
    )(part)


def reduce_kernel(groups, owners, src, out, first, first_sum, second, second_sum, third, mine,
                  core_sems, pair_sems, row_sems, all_sems):
    dp, me = lax.axis_index("dp"), lax.axis_index("bucket")
    halves = groups // 2
    core, side = lax.rem(dp, 2), dp // 2
    chunk = core * halves + side
    partner = side * 2 + (1 - core)
    barrier = pltpu.get_barrier_semaphore()

    def group_peer(i):
        return lax.rem(dp + i, groups)

    def owner_peer(i):
        return lax.rem(me + i, owners)

    def greet_group(i, carry):
        pl.semaphore_signal(barrier, inc=1, device_id=(group_peer(i), me), device_id_type=MESH)
        return carry

    def greet_owner(i, carry):
        pl.semaphore_signal(barrier, inc=1, device_id=(dp, owner_peer(i)), device_id_type=MESH)
        return carry

    lax.fori_loop(1, groups, greet_group, 0)
    lax.fori_loop(1, owners, greet_owner, 0)
    pl.semaphore_wait(barrier, groups + owners - 2)

    def remote(source, target, sems, i, j, device):
        return pltpu.make_async_remote_copy(
            src_ref=source,
            dst_ref=target,
            send_sem=sems.at[0, i],
            recv_sem=sems.at[1, j],
            device_id=device,
            device_id_type=MESH,
        )

    def bucket_of(i):
        return lax.rem(me + 1 + i, owners)

    def swap(i):
        bucket = bucket_of(i)
        return remote(src.at[bucket, 1 - core], first.at[bucket], core_sems, i, i, (partner, me))

    def to_side(i, n, arriving):
        bucket = bucket_of(i)
        other = lax.rem(side + n, halves)
        slot = other if arriving else side
        return remote(
            first_sum.at[bucket, other], second.at[slot, bucket], pair_sems,
            n * owners + i, slot * owners + i, (other * 2 + core, me),
        )

    def to_owner(i, arriving):
        other = owner_peer(i)
        slot = other if arriving else me
        return remote(second_sum.at[other], third.at[slot], row_sems, i, slot, (dp, other))

    def start_swap(i, carry):
        swap(i).start()
        return carry

    def add_first(i, carry):
        bucket = bucket_of(i)
        swap(i).wait_recv()
        total = src[bucket, core].astype(jnp.float32) + first[bucket].astype(jnp.float32)
        first_sum[bucket] = total.astype(jnp.bfloat16)
        for n in range(1, halves):
            to_side(i, n, False).start()
        return carry

    def add_second(i, carry):
        bucket = bucket_of(i)
        total = first_sum[bucket, side].astype(jnp.float32)
        for n in range(1, halves):
            to_side(i, n, True).wait_recv()
            total = total + second[lax.rem(side + n, halves), bucket].astype(jnp.float32)
        second_sum[bucket] = total.astype(jnp.bfloat16)
        return carry

    def add_and_send(i, carry):
        add_second(i, carry)
        to_owner(i + 1, False).start()
        return carry

    def wait_owner(i, carry):
        to_owner(i, True).wait_recv()
        return carry

    lax.fori_loop(0, owners, start_swap, 0)
    lax.fori_loop(0, owners, add_first, 0)
    lax.fori_loop(0, owners - 1, add_and_send, 0)
    add_second(owners - 1, 0)
    third[me] = second_sum[me]
    lax.fori_loop(1, owners, wait_owner, 0)
    total = lax.fori_loop(
        1, owners, lambda i, t: t + third[i].astype(jnp.float32), third[0].astype(jnp.float32)
    )
    mine[...] = total.astype(jnp.bfloat16)

    def to_group(i, arriving):
        other = group_peer(i)
        device = other if arriving else dp
        slot = lax.rem(device, 2) * halves + device // 2
        return remote(mine, out.at[slot], all_sems, i, slot, (other, me))

    def send_group(i, carry):
        to_group(i, False).start()
        return carry

    def wait_group(i, carry):
        to_group(i, True).wait_recv()
        return carry

    lax.fori_loop(1, groups, send_group, 0)
    out[chunk] = mine[...]
    lax.fori_loop(1, groups, wait_group, 0)

    def sent_owner(i, carry):
        to_owner(i, False).wait_send()
        return carry

    def sent_group(i, carry):
        to_group(i, False).wait_send()
        return carry

    def sent_first(i, carry):
        swap(i).wait_send()
        for n in range(1, halves):
            to_side(i, n, False).wait_send()
        return carry

    lax.fori_loop(0, owners, sent_first, 0)
    lax.fori_loop(1, owners, sent_owner, 0)
    lax.fori_loop(1, groups, sent_group, 0)


def reduce_rows(packed, collective_id):
    groups, owners = lax.axis_size("dp"), lax.axis_size("bucket")
    halves = groups // 2
    rows = packed.shape[1] // groups
    source = packed.reshape(owners, 2, halves, rows, LANES)
    kind = jnp.bfloat16
    return pl.pallas_call(
        functools.partial(reduce_kernel, groups, owners),
        out_shape=jax.ShapeDtypeStruct((groups, rows, LANES), kind),
        in_specs=[pl.BlockSpec(memory_space=pltpu.VMEM)],
        out_specs=pl.BlockSpec(memory_space=pltpu.VMEM),
        scratch_shapes=[
            pltpu.VMEM((owners, halves, rows, LANES), kind),
            pltpu.VMEM((owners, halves, rows, LANES), kind),
            pltpu.VMEM((halves, owners, rows, LANES), kind),
            pltpu.VMEM((owners, rows, LANES), kind),
            pltpu.VMEM((owners, rows, LANES), kind),
            pltpu.VMEM((rows, LANES), kind),
            pltpu.SemaphoreType.DMA((2, owners)),
            pltpu.SemaphoreType.DMA((2, halves * owners)),
            pltpu.SemaphoreType.DMA((2, owners)),
            pltpu.SemaphoreType.DMA((2, groups)),
        ],
        compiler_params=pltpu.CompilerParams(
            collective_id=collective_id, has_side_effects=True, vmem_limit_bytes=16 << 20
        ),
        cost_estimate=pl.CostEstimate(flops=10**7, bytes_accessed=6 * 10**7, transcendentals=0),
        name="reduce_rows",
    )(source)


def in_hbm(array):
    return pltpu.with_memory_space_constraint(array, pltpu.HBM)


def local(frames, lengths, owners, upstream, ln_gain, w_in, w_dw, bn_gain, bn_bias, w_out):
    loaders = lax.axis_size("bucket")
    width = frames.shape[1]
    taps = w_dw.shape[1]
    slot_count = lengths.shape[1] // loaders
    span = frames.shape[0] // slot_count
    pair_count = slot_count // loaders
    own_rows = upstream.shape[0]
    blocks = width // LANES
    total_frames = float(own_rows * loaders * lax.axis_size("dp"))
    stage_shape = pltpu.VMEM((blocks, own_rows + span, LANES), jnp.float32)
    slot_shape = jax.ShapeDtypeStruct((slot_count, span, width), jnp.bfloat16)
    in_vmem = pl.BlockSpec(memory_space=pltpu.VMEM)
    in_smem = pl.BlockSpec(memory_space=pltpu.SMEM)
    outgoing, meta = pl.pallas_call(
        functools.partial(plan_kernel, slot_count),
        in_specs=[in_smem, in_smem, in_vmem],
        out_specs=[in_vmem, in_smem],
        out_shape=[slot_shape, jax.ShapeDtypeStruct((3, slot_count), jnp.int32)],
        scratch_shapes=[
            stage_shape,
            pltpu.SMEM((loaders,), jnp.int32),
            pltpu.SMEM((slot_count + 1,), jnp.int32),
        ],
        compiler_params=pltpu.CompilerParams(vmem_limit_bytes=VMEM_LIMIT),
        name="plan",
    )(in_hbm(lengths), in_hbm(owners), in_hbm(upstream))

    def exchange(slots):
        slots = slots.reshape(loaders, pair_count, span, width)
        moved = lax.all_to_all(slots, "bucket", split_axis=0, concat_axis=0, tiled=True)
        return moved.reshape(slot_count, span, width)

    incoming = exchange(outgoing)

    group = 4
    steps = slot_count // group
    rows = group * span
    row_block = pl.BlockSpec((rows, width), lambda i, *_: (i, 0))
    all_rows = slot_count * span
    gain_row, bn_gain_row, bn_bias_row = ln_gain[None], bn_gain[None], bn_bias[None]
    w_taps = jnp.pad(w_dw.T, ((0, 1), (0, 0)))
    sums_shape = (2 * blocks, LANES)
    params = pltpu.CompilerParams(
        dimension_semantics=("arbitrary",), vmem_limit_bytes=VMEM_LIMIT
    )
    padded_shape = pltpu.VMEM((group, blocks, span, LANES), jnp.float32)

    thin_block = pl.BlockSpec((rows, LANES), lambda i, *_: (i, 0))
    tall = pltpu.HBM((all_rows, width), jnp.float32)
    conv, part, normed, inverse, linear, gate = pl.pallas_call(
        functools.partial(forward_kernel, group, span, taps),
        grid_spec=pltpu.PrefetchScalarGridSpec(
            num_scalar_prefetch=1,
            grid=(steps,),
            in_specs=[row_block, whole((1, width)), whole(w_in.shape), whole(w_taps.shape)],
            out_specs=[
                row_block, whole(sums_shape), row_block, thin_block, row_block, row_block
            ],
            scratch_shapes=[padded_shape],
        ),
        out_shape=[
            tall,
            jax.ShapeDtypeStruct(sums_shape, jnp.float32),
            tall,
            pltpu.HBM((all_rows, LANES), jnp.float32),
            tall,
            tall,
        ],
        compiler_params=params,
        cost_estimate=pl.CostEstimate(
            flops=2 * 10**9, bytes_accessed=4 * 10**7, transcendentals=0
        ),
        name="forward",
    )(meta, frames, gain_row, w_in, w_taps)
    totals = sum_everywhere(part, 0)

    out_rows, grad_bn, back_part, grad_wout = pl.pallas_call(
        functools.partial(middle_kernel, group, span, total_frames),
        grid_spec=pltpu.PrefetchScalarGridSpec(
            num_scalar_prefetch=1,
            grid=(steps,),
            in_specs=[
                row_block, whole(slot_shape.shape), whole(sums_shape), whole((1, width)),
                whole((1, width)), whole(w_out.shape),
            ],
            out_specs=[whole(slot_shape.shape), row_block, whole(sums_shape), whole(w_out.shape)],
        ),
        out_shape=[
            slot_shape,
            tall,
            jax.ShapeDtypeStruct(sums_shape, jnp.float32),
            pltpu.HBM(w_out.shape, jnp.float32),
        ],
        compiler_params=params,
        cost_estimate=pl.CostEstimate(
            flops=3 * 10**9, bytes_accessed=2 * 10**7, transcendentals=0
        ),
        name="middle",
    )(meta, in_hbm(conv), incoming, totals, bn_gain_row, bn_bias_row, w_out)

    back_totals = sum_everywhere(back_part, 1)
    leaving, back_totals = lax.optimization_barrier((out_rows, back_totals))
    arrived = exchange(leaving)

    share = width // loaders
    packed_rows = (w_in.shape[1] // LANES + blocks + 1) * share
    grad_frames, packed = pl.pallas_call(
        functools.partial(backward_kernel, group, span, taps, total_frames),
        grid_spec=pltpu.PrefetchScalarGridSpec(
            num_scalar_prefetch=1,
            grid=(steps,),
            in_specs=[
                row_block, thin_block, row_block, row_block, row_block, row_block,
                whole(sums_shape), whole(sums_shape),
                whole((1, width)), whole((1, width)), whole(w_in.shape), whole(w_taps.shape),
                whole(w_out.shape),
            ],
            out_specs=[row_block, whole((loaders, packed_rows, LANES))],
            scratch_shapes=[
                padded_shape,
                padded_shape,
                pltpu.VMEM((rows, width), jnp.float32),
                pltpu.VMEM((blocks, taps + 1, SUB, LANES), jnp.float32),
                pltpu.VMEM(w_in.shape, jnp.float32),
                pltpu.VMEM((1, width), jnp.float32),
                pltpu.VMEM((LANES, LANES), jnp.float32),
            ],
        ),
        out_shape=[
            jax.ShapeDtypeStruct((all_rows, width), jnp.bfloat16),
            jax.ShapeDtypeStruct((loaders, packed_rows, LANES), jnp.bfloat16),
        ],
        compiler_params=params,
        cost_estimate=pl.CostEstimate(
            flops=6 * 10**9, bytes_accessed=8 * 10**7, transcendentals=0
        ),
        name="backward",
    )(
        meta, *map(in_hbm, (normed, inverse, linear, gate, conv, grad_bn)), totals, back_totals, gain_row, bn_gain_row, w_in, w_taps,
        in_hbm(grad_wout),
    )
    reduced = reduce_rows(packed, 2).reshape(-1, share, LANES)
    out_frames, grad_win, grad_wo, last = pl.pallas_call(
        finish_kernel,
        in_specs=[in_smem, in_vmem, in_vmem],
        out_specs=[in_vmem] * 4,
        out_shape=[
            jax.ShapeDtypeStruct((own_rows, width), jnp.bfloat16),
            jax.ShapeDtypeStruct((share, w_in.shape[1]), jnp.float32),
            jax.ShapeDtypeStruct((share, width), jnp.float32),
            jax.ShapeDtypeStruct((share, LANES), jnp.float32),
        ],
        scratch_shapes=[stage_shape],
        compiler_params=pltpu.CompilerParams(vmem_limit_bytes=VMEM_LIMIT),
        name="finish",
    )(meta, arrived, reduced)
    flat_back = back_totals.reshape(2, width)
    return (
        out_frames,
        grad_frames,
        grad_win,
        grad_wo,
        last[:, :taps],
        last[:, taps],
        flat_back[1],
        flat_back[0],
    )


def solution(mesh):
    placed = (
        P(("dp", "bucket"), None),
        P("dp", None),
        P("dp", None),
        P(("dp", "bucket"), None),
        P(),
        P(),
        P(),
        P(),
        P(),
        P(),
    )
    return jax.shard_map(
        local,
        mesh=mesh,
        in_specs=placed,
        out_specs=(
            P(("dp", "bucket"), None),
            P(("dp", "bucket"), None),
            P("bucket", None),
            P("bucket", None),
            P("bucket", None),
            P("bucket"),
            P(),
            P(),
        ),
        check_vma=False,
    )
```

profile of v0, /device:TPU:0, one launch (start us, length us, event | category | flops | bytes accessed | tf_op | source)
XLA Modules:
  0.0 135.0 jit_solution(869210817985733074)
XLA Ops:
  0.6 4.0 %plan.1 = (bf16[32,48,512]{2,1,0:T(8,128)(2,1)}, s32[3,32]{1,0:T(4,128)S(1)}) custom-call(s32[1,256]{1,0:T(1,128)} %lens_ref.1, s32[1,256]{1,0:T(1,128)} %owners_ref.1, bf16[768,512]{1,0:T(8,128)(2,1)} %up_ref.1), custom_call_target="tpu_custom_call" | custom-call | tf_op jit(solution)/shard_map/plan/pallas_call | solution.py:608
  4.6 0.0 copy-start.7
  4.6 0.0 copy-start
  4.6 0.0 copy-start.5
  4.6 7.4 %all-to-all-start = ((bf16[8,4,48,512]{3,2,1,0:T(8,128)(2,1)}), bf16[8,4,48,512]{3,2,1,0:T(8,128)(2,1)S(1)}, u32[]{:S(2)}, u32[]{:S(2)}) async-start(bf16[8,4,48,512]{3,2,1,0:T(8,128)(2,1)} %bitcast.2), calls=%async_computation | async-start | bytes 3145728 | tf_op jit(solution)/shard_map/all_to_all | solution.py:624
  12.1 0.0 copy-done.7
  12.1 0.0 copy-done
  12.1 0.0 copy-done.5
  12.1 0.0 copy-start.1
  12.1 1.2 copy-done.1
  13.3 0.0 copy-start.4
  13.3 0.0 copy-start.6
  13.3 15.1 %forward.1 = (f32[1536,512]{1,0:T(8,128)}, f32[8,128]{1,0:T(8,128)S(1)}, f32[1536,512]{1,0:T(8,128)}, f32[1536,128]{1,0:T(8,128)}, f32[1536,512]{1,0:T(8,128)}, /*index=5*/f32[1536,512]{1,0:T(8,128)}) custom-call(s32[3,32]{1,0:T(4,128)S(1)} %get-tuple-element.28.lens_ref.meta_ref, bf16[1536,512]{1,0:T(8,128)(2,1)S(1)} %copy-done, f32[1,512]{1,0:T(1,128)S(1)} %bitcast.21, ...), custom_call_target="tpu_custom_call" | custom-call | flops 2000000000 | bytes 40000000 | tf_op jit(solution)/shard_map/forward/pallas_call | solution.py:644
  28.4 25.8 %sum_everywhere_0.1.total_ref = f32[8,128]{1,0:T(8,128)S(1)} custom-call(f32[8,128]{1,0:T(8,128)S(1)} %get-tuple-element.31.part_ref), custom_call_target="tpu_custom_call" | custom-call | flops 1000000 | bytes 20000000 | tf_op jit(solution)/shard_map/sum_everywhere_0/pallas_call | solution.py:404
  54.2 0.0 all-to-all-done
  54.2 0.0 copy-done.4
  54.2 0.0 copy-done.6
  54.2 0.0 copy-start.3
  54.2 1.0 copy-done.3
  55.2 9.6 %middle.1 = (bf16[32,48,512]{2,1,0:T(8,128)(2,1)}, f32[1536,512]{1,0:T(8,128)}, f32[8,128]{1,0:T(8,128)S(1)}, f32[512,512]{1,0:T(8,128)}) custom-call(s32[3,32]{1,0:T(4,128)S(1)} %get-tuple-element.28.lens_ref.meta_ref, f32[1536,512]{1,0:T(8,128)} %get-tuple-element.29.conv_ref, bf16[32,48,512]{2,1,0:T(8,128)(2,1)S(1)} %bitcast.17, ...), custom_call_target="tpu_custom_call" | custom-call | flops 3000000000 | bytes 20000000 | tf_op jit(solution)/shard_map/middle/pallas_call | solution.py:671
  64.8 0.0 copy-start.2
  64.8 9.7 %sum_everywhere_1.1.back_ref = f32[8,128]{1,0:T(8,128)S(1)} custom-call(f32[8,128]{1,0:T(8,128)S(1)} %get-tuple-element.33.part_ref), custom_call_target="tpu_custom_call" | custom-call | flops 1000000 | bytes 20000000 | tf_op jit(solution)/shard_map/sum_everywhere_1/pallas_call | solution.py:404
  74.6 3.8 %all-to-all-start.1 = ((bf16[8,4,48,512]{3,2,1,0:T(8,128)(2,1)}), bf16[8,4,48,512]{3,2,1,0:T(8,128)(2,1)S(1)}, u32[]{:S(2)}, u32[]{:S(2)}) async-start(bf16[8,4,48,512]{3,2,1,0:T(8,128)(2,1)} %bitcast.6), calls=%async_computation.1 | async-start | bytes 3145728 | tf_op jit(solution)/shard_map/all_to_all | solution.py:624
  78.4 0.0 copy-done.2
  78.4 29.1 %backward.1 = (bf16[1536,512]{1,0:T(8,128)(2,1)}, bf16[8,832,128]{2,1,0:T(8,128)(2,1)S(1)}) custom-call(s32[3,32]{1,0:T(4,128)S(1)} %get-tuple-element.28.lens_ref.meta_ref, f32[1536,512]{1,0:T(8,128)} %get-tuple-element.35.normed_ref, f32[1536,128]{1,0:T(8,128)} %get-tuple-element.36.inverse_ref, f32[1536,512]{1,0:T(8,128)} %get-tuple-element.37.linear_ref, ...), custom_call_target="tpu_custom_call" | custom-call | flops 6000000000 | bytes 80000000 | tf_op jit(solution)/shard_map/backward/pallas_call | solution.py:701
  107.5 23.5 %reduce_rows.1 = bf16[4,208,128]{2,1,0:T(8,128)(2,1)S(1)} custom-call(bf16[8,2,2,208,128]{4,3,2,1,0:T(8,128)(2,1)S(1)} %bitcast.16), custom_call_target="tpu_custom_call" | custom-call | flops 10000000 | bytes 60000000 | tf_op jit(solution)/shard_map/reduce_rows/pallas_call | solution.py:565
  131.0 0.6 slice_bitcast_fusion
  131.6 0.0 all-to-all-done.1
  131.6 2.0 %finish.1 = (bf16[768,512]{1,0:T(8,128)(2,1)}, f32[64,1024]{1,0:T(8,128)}, f32[64,512]{1,0:T(8,128)}, f32[64,128]{1,0:T(8,128)S(1)}) custom-call(s32[3,32]{1,0:T(4,128)S(1)} %get-tuple-element.28.lens_ref.meta_ref, bf16[32,48,512]{2,1,0:T(8,128)(2,1)S(1)} %bitcast.15, bf16[13,64,128]{2,1,0:T(8,128)(2,1)S(1)} %bitcast.18), custom_call_target="tpu_custom_call" | custom-call | tf_op jit(solution)/shard_map/finish/pallas_call | solution.py:737
  133.7 0.7 slice_reduce_fusion
  134.3 0.7 copy.19
  (1 shorter events, 0.0 us)
Async XLA Ops:
  4.6 7.5 %copy-start.7 = (f32[512,31]{0,1:T(8,128)S(1)}, f32[512,31]{0,1:T(8,128)}, u32[]{:S(2)}) copy-start(f32[512,31]{0,1:T(8,128)} %param.16) | copy-start | bytes 190468
  4.6 7.5 %copy-start = (bf16[1536,512]{1,0:T(8,128)(2,1)S(1)}, bf16[1536,512]{1,0:T(8,128)(2,1)}, u32[]{:S(2)}) copy-start(bf16[1536,512]{1,0:T(8,128)(2,1)} %frames_ref.1) | copy-start | bytes 4718596
  4.6 7.5 %copy-start.5 = (f32[512]{0:T(512)S(1)}, f32[512]{0:T(512)}, u32[]{:S(2)}) copy-start(f32[512]{0:T(512)} %param.14) | copy-start | bytes 6148
  4.6 49.5 %all-to-all-start = ((bf16[8,4,48,512]{3,2,1,0:T(8,128)(2,1)}), bf16[8,4,48,512]{3,2,1,0:T(8,128)(2,1)S(1)}, u32[]{:S(2)}, u32[]{:S(2)}) async-start(bf16[8,4,48,512]{3,2,1,0:T(8,128)(2,1)} %bitcast.2), calls=%async_computation | async-start | bytes 3145728 | tf_op jit(solution)/shard_map/all_to_all | solution.py:624
  12.1 1.2 copy-start.1
  13.3 40.9 %copy-start.4 = (f32[512]{0:T(512)S(1)}, f32[512]{0:T(512)}, u32[]{:S(2)}) copy-start(f32[512]{0:T(512)} %param.18) | copy-start | bytes 6148
  13.3 40.9 %copy-start.6 = (f32[512]{0:T(512)S(1)}, f32[512]{0:T(512)}, u32[]{:S(2)}) copy-start(f32[512]{0:T(512)} %param.17) | copy-start | bytes 6148
  54.2 1.0 copy-start.3
  64.8 13.5 %copy-start.2 = (bf16[512,1024]{1,0:T(8,128)(2,1)S(1)}, bf16[512,1024]{1,0:T(8,128)(2,1)}, u32[]{:S(2)}) copy-start(bf16[512,1024]{1,0:T(8,128)(2,1)} %w_in_ref.3) | copy-start | bytes 3145732
  74.6 57.0 %all-to-all-start.1 = ((bf16[8,4,48,512]{3,2,1,0:T(8,128)(2,1)}), bf16[8,4,48,512]{3,2,1,0:T(8,128)(2,1)S(1)}, u32[]{:S(2)}, u32[]{:S(2)}) async-start(bf16[8,4,48,512]{3,2,1,0:T(8,128)(2,1)} %bitcast.6), calls=%async_computation.1 | async-start | bytes 3145728 | tf_op jit(solution)/shard_map/all_to_all | solution.py:624
where the time goes:
time: 136 us; the launch traced here: 135 us
  Pallas kernels  119 us (88%)
  starting transfers between devices  11.2 us (8%)
  local copies, waits for them, and re-layouts  4.26 us (3%)
    pallas_call x2, Pallas kernels, sum_everywhere(): pl.pallas_call(functools.partial(sum_kernel, groups, owners), out_shape=j...  35.5 us
    pallas_call x1, Pallas kernels, local(): pl.pallas_call(functools.partial(backward_kernel, group, span, taps, tota...  29.1 us
    pallas_call x1, Pallas kernels, reduce_rows(): pl.pallas_call(functools.partial(reduce_kernel, groups, owners), out_shap...  23.5 us
    pallas_call x1, Pallas kernels, local(): pl.pallas_call(functools.partial(forward_kernel, group, span, taps), grid...  15.1 us
    all_to_all x2, starting transfers between devices, exchange(): lax.all_to_all(slots, 'bucket', split_axis=0, concat_axis=0, tiled=True)  11.2 us
    pallas_call x1, Pallas kernels, local(): pl.pallas_call(functools.partial(middle_kernel, group, span, total_frames...  9.6 us
    pallas_call x1, Pallas kernels, local(): pl.pallas_call(functools.partial(plan_kernel, slot_count), in_specs=[in_s...  3.96 us
    unnamed x17, local copies, waits for them, and re-layouts  2.97 us
  transfers between devices with their start and end apart: 2, of which 0 were waited for; matrix products, arithmetic and copies ran while one was open for 0% of the time, Pallas kernels for 69%

commit v1 on v0

v1 whole, which is shorter than its diff:
```python
import functools

import jax
import jax.numpy as jnp
import numpy as np
from jax import lax
from jax.experimental import pallas as pl
from jax.experimental.pallas import tpu as pltpu
from jax.sharding import PartitionSpec as P

EPSILON = 1e-05
LANES = 128
SUB = 8
PACK = 16
MESH = pl.DeviceIdType.MESH
BF16 = jnp.bfloat16
F32 = jnp.float32


def lane(c):
    return slice(c * LANES, (c + 1) * LANES)


def row_of(packed, first, blocks):
    return jnp.concatenate([packed[first + c : first + c + 1] for c in range(blocks)], axis=1)


def keep_live(values, lengths, span):
    position = lax.broadcasted_iota(jnp.int32, (span, values.shape[1]), 0)
    parts = [
        jnp.where(position < length, values[i * span : (i + 1) * span], 0.0)
        for i, length in enumerate(lengths)
    ]
    return jnp.concatenate(parts, axis=0)


def fold_rows(values):
    rows, width = values.shape
    return jnp.sum(values.reshape(rows // SUB, SUB, width), axis=0)


def matmul(a, b):
    return jnp.dot(a, b, preferred_element_type=F32)


def matmul_nt(a, b):
    return lax.dot_general(a, b, (((1,), (1,)), ((), ())), preferred_element_type=F32)


def matmul_tn(a, b):
    return lax.dot_general(a, b, (((0,), (0,)), ((), ())), preferred_element_type=F32)


def matmul_exact(a, b):
    return jnp.dot(a, b, preferred_element_type=F32, precision=lax.Precision.HIGHEST)


def transform_tables(span, taps, group):
    size = -(-(span + taps // 2) // (2 * PACK)) * (2 * PACK)
    half = size // 2
    freq = np.arange(half)[:, None]

    def angle(times):
        return 2.0 * np.pi * freq * np.asarray(times)[None, :] / size

    def flip(times):
        return np.where(np.asarray(times) % 2 == 0, 1.0, -1.0)

    times = np.arange(span)
    real, imag = np.cos(angle(times)), -np.sin(angle(times))
    imag[0] = flip(times)
    forward = np.concatenate([real, imag], axis=0)
    scale = np.where(np.arange(size) % half == 0, 1.0, 2.0) / size
    inverse = (forward * scale[:, None]).T
    lags = taps // 2 - np.arange(taps)
    wr, wi, wn = np.cos(angle(lags)), -np.sin(angle(lags)), np.cos(angle(lags))
    wi[0] = 0.0
    wn[0] = flip(lags)
    spectrum = np.concatenate([wr, wi, wn], axis=0)
    spectrum = np.pad(spectrum, ((0, 0), (0, 1)))
    back = -lags
    cr, cn, ci = np.cos(angle(back)), np.cos(angle(back)), -np.sin(angle(back))
    cn[0] = flip(back)
    ci[0] = 0.0
    both = np.concatenate([scale[:half], scale[half:], scale[half:]])
    correlate = (np.concatenate([cr, cn, ci], axis=0) * both[:, None]).T
    correlate = np.pad(correlate, ((0, 1), (0, 0)))
    eye = np.eye(group)
    return (
        size,
        jnp.asarray(np.kron(eye, forward), BF16),
        jnp.asarray(np.kron(eye, inverse), BF16),
        jnp.asarray(spectrum, F32),
        jnp.asarray(correlate, F32),
    )


def tables_kernel(slots, lens_ref, owners_ref, meta_ref, counts):
    me = lax.axis_index("bucket")
    loaders = lens_ref.shape[1] // slots
    pairs = slots // loaders

    def look(i, carry):
        found, start = carry
        for j in range(SUB):
            at = i * SUB + j
            mine = owners_ref[0, at] == me
            meta_ref[2, found] = start
            found = found + jnp.where(mine, 1, 0)
            start = start + jnp.where(mine, lens_ref[0, at], 0)
        return found, start

    lax.fori_loop(0, loaders * slots // SUB, look, (jnp.int32(0), jnp.int32(0)))

    def clear(i, carry):
        counts[i] = 0
        return carry

    lax.fori_loop(0, loaders, clear, 0)

    def place(i, carry):
        owner = owners_ref[0, me * slots + i]
        rank = counts[owner]
        counts[owner] = rank + 1
        at = owner * pairs + rank
        meta_ref[0, at] = lens_ref[0, me * slots + i]
        meta_ref[1, at] = i
        return carry

    lax.fori_loop(0, slots, place, 0)


def step_kernel(
    groups, owners, group, taps, size, early, total_frames,
    meta, frames_hbm, up_hbm, w_in_hbm, w_out_hbm, gain_ref, bn_gain_ref, bn_bias_ref, w_taps_ref,
    fwd_ref, inv_ref, spec_ref, corr_ref,
    grads_ref, arrived_ref, reduced_ref, back_ref, ln_ref,
    frames, up, w_in_ref, w_out_ref, stage, outgoing, arrive, outbuf,
    normed_s, inverse_s, linear_s, gate_s, h_s, spect_s, conv_s, fac_s, sw_s, dy_s, ga_s,
    wspec, acc, xacc, tot, parts, slots_s, flat,
    packed, first, first_sum, second, second_sum, third, mine,
    local_sems, sum_send, sum_recv, up_send, up_recv, out_send, out_recv,
    core_sems, pair_sems, row_sems, all_sems,
):
    dp, me = lax.axis_index("dp"), lax.axis_index("bucket")
    slot_count, span, width = frames.shape
    all_rows = slot_count * span
    own_rows = up.shape[0]
    blocks = width // LANES
    wide = w_in_ref.shape[1] // LANES
    chunk = all_rows // owners
    pairs = slot_count // owners
    steps = slot_count // group
    held = group // pairs
    grows = group * span
    half = size // 2
    count = groups * owners
    rank = dp * owners + me
    barrier = pltpu.get_barrier_semaphore()

    def device_of(i):
        other = lax.rem(rank + i, count)
        return (other // owners, lax.rem(other, owners))

    def greet(i, carry):
        pl.semaphore_signal(barrier, inc=1, device_id=device_of(i), device_id_type=MESH)
        return carry

    lax.fori_loop(1, count, greet, 0)
    loads = [
        pltpu.make_async_copy(source, target, local_sems.at[n])
        for n, (source, target) in enumerate(
            ((up_hbm, up), (frames_hbm, frames), (w_in_hbm, w_in_ref), (w_out_hbm, w_out_ref))
        )
    ]
    for load in loads:
        load.start()

    loads[0].wait()
    for c in range(blocks):
        stage[c, :own_rows] = up[:, lane(c)].astype(F32)
        stage[c, own_rows:] = jnp.zeros((span, LANES), F32)

    def lay_out(b, carry):
        for q in range(pairs):
            start = meta[2, b * pairs + q]
            for c in range(blocks):
                outgoing[b, q * span : (q + 1) * span, lane(c)] = stage[
                    c, pl.ds(start, span)
                ].astype(BF16)
        return carry

    lax.fori_loop(0, owners, lay_out, 0)
    arrive[me] = outgoing[me]

    def offset_of(j):
        return lax.rem(owners // 2 + j, owners) + (j // (owners - owners // 2))

    def up_copy(j, part, arriving):
        offset = offset_of(j)
        target = lax.rem(me + offset, owners)
        slot = lax.rem(me + owners - offset, owners) if arriving else me
        rows = pl.ds(0, early) if part == 0 else pl.ds(early, chunk - early)
        return pltpu.make_async_remote_copy(
            src_ref=outgoing.at[target, rows],
            dst_ref=arrive.at[slot, rows],
            send_sem=up_send.at[part, j],
            recv_sem=up_recv.at[part, j],
            device_id=(dp, target),
            device_id_type=MESH,
        )

    def start_up(part):
        def body(j, carry):
            up_copy(j, part, False).start()
            return carry

        lax.fori_loop(0, owners - 1, body, 0)

    def out_copy(j, arriving):
        offset = offset_of(j)
        target = lax.rem(me + offset, owners)
        slot = lax.rem(me + owners - offset, owners) if arriving else me
        return pltpu.make_async_remote_copy(
            src_ref=outbuf.at[target],
            dst_ref=arrived_ref.at[slot],
            send_sem=out_send.at[j],
            recv_sem=out_recv.at[j],
            device_id=(dp, target),
            device_id_type=MESH,
        )

    def sum_copy(n, i, slot):
        return pltpu.make_async_remote_copy(
            src_ref=parts.at[n],
            dst_ref=slots_s.at[n, slot],
            send_sem=sum_send.at[n, i],
            recv_sem=sum_recv.at[n, slot],
            device_id=device_of(i),
            device_id_type=MESH,
        )

    def sum_start(n):
        def send(i, carry):
            sum_copy(n, i, rank).start()
            return carry

        lax.fori_loop(1, count, send, 0)
        slots_s[n, rank] = parts[n]

    def sum_finish(n):
        def receive(i, carry):
            sum_copy(n, i, lax.rem(rank + i, count)).wait_recv()
            return carry

        lax.fori_loop(1, count, receive, 0)
        return lax.fori_loop(
            1, count, lambda i, total: total + slots_s[n, i], slots_s[n, 0]
        )

    def gather_parts(n):
        for k in range(2):
            row = jnp.sum(acc[k], axis=0, keepdims=True)
            for c in range(blocks):
                parts[n, k * blocks + c : k * blocks + c + 1] = row[:, lane(c)]

    wspec[...] = matmul_exact(spec_ref[...], w_taps_ref[...])
    acc[...] = jnp.zeros_like(acc)
    pl.semaphore_wait(barrier, count - 1)
    start_up(0)
    loads[1].wait()
    loads[2].wait()

    def rows_of(i):
        return pl.ds(pl.multiple_of(i * grows, PACK), grows)

    def spec_rows(i):
        return pl.ds(pl.multiple_of(i * group * size, PACK), group * size)

    def lengths_of(i):
        return [meta[0, i * group + u] for u in range(group)]

    def forward(i, carry):
        rows = rows_of(i)
        lengths = lengths_of(i)
        values = jnp.concatenate(
            [frames[meta[1, i * group + u]] for u in range(group)], axis=0
        ).astype(F32)
        centred = values - jnp.mean(values, axis=1, keepdims=True)
        inverse = lax.rsqrt(jnp.mean(centred * centred, axis=1, keepdims=True) + EPSILON)
        normed = centred * inverse
        h = (normed * gain_ref[...]).astype(BF16)
        projected = matmul(h, w_in_ref[...])
        linear, gate = projected[:, :width], jax.nn.sigmoid(projected[:, width:])
        normed_s[rows] = normed
        inverse_s[rows] = jnp.broadcast_to(inverse, (grows, LANES))
        linear_s[rows] = linear
        gate_s[rows] = gate
        h_s[rows] = h
        gated = keep_live(linear * gate, lengths, span).astype(BF16)
        spect = matmul(fwd_ref[...], gated)
        spect_s[spec_rows(i)] = spect
        wr, wi, wn = wspec[:half], wspec[half : 2 * half], wspec[2 * half :]
        mixed = []
        for u in range(group):
            re = spect[u * size : u * size + half]
            im = spect[u * size + half : (u + 1) * size]
            mixed.append((wr * re - wi * im).astype(BF16))
            mixed.append((wn * im + wi * re).astype(BF16))
        conv = matmul(inv_ref[...], jnp.concatenate(mixed, axis=0))
        conv_s[rows] = conv
        masked = keep_live(conv, lengths, span)
        acc[0] += fold_rows(masked)
        acc[1] += fold_rows(masked * masked)
        return carry

    lax.fori_loop(0, steps, forward, 0)
    gather_parts(0)
    sum_start(0)
    start_up(1)
    loads[3].wait()
    tot[...] = sum_finish(0)
    centre = row_of(tot, 0, blocks) / total_frames
    variance = row_of(tot, blocks, blocks) / total_frames - centre * centre
    bn_inverse = lax.rsqrt(variance + EPSILON)
    acc[...] = jnp.zeros_like(acc)
    bn_gain, bn_bias = bn_gain_ref[...], bn_bias_ref[...]

    def swish(i, carry):
        rows = rows_of(i)
        bn_normed = (conv_s[rows] - centre) * bn_inverse
        conv_s[rows] = bn_normed
        bn = bn_normed * bn_gain + bn_bias
        sig = jax.nn.sigmoid(bn)
        swished = (bn * sig).astype(BF16)
        sw_s[rows] = swished
        fac_s[rows] = sig * (1.0 + bn * (1.0 - sig))
        out = matmul(swished, w_out_ref[...]).astype(BF16)
        for r in range(held):
            outbuf[i * held + r] = out[r * chunk : (r + 1) * chunk]
        return carry

    lax.fori_loop(0, steps, swish, 0)
    my_step = me // held

    def middle(t, carry):
        late = lax.rem(t + steps - 1, steps)
        offset = lax.rem(steps // 2 + late, steps) + (late // (steps - steps // 2))
        i = lax.rem(my_step + 2 * steps - offset * ((t + steps - 1) // steps), steps)
        rows = rows_of(i)
        lengths = lengths_of(i)
        for r in range(held):
            owner = i * held + r

            @pl.when(owner != me)
            def _():
                gap = lax.rem(me + owners - owner, owners)
                j = lax.rem(gap + owners - owners // 2, owners) - (
                    (owners // 2 - 1 + owners - gap) // owners
                )
                up_copy(j, 0, True).wait_recv()
                up_copy(j, 1, True).wait_recv()

        arrived = jnp.concatenate([arrive[i * held + r] for r in range(held)], axis=0)
        dy = keep_live(arrived.astype(F32), lengths, span).astype(BF16)
        dy_s[rows] = dy
        grad_bn = matmul_nt(dy, w_out_ref[...]) * fac_s[rows]
        fac_s[rows] = grad_bn
        acc[0] += fold_rows(grad_bn)
        acc[1] += fold_rows(grad_bn * conv_s[rows])
        return carry

    lax.fori_loop(0, steps, middle, 0)
    gather_parts(1)
    sum_start(1)

    def start_out(j, carry):
        out_copy(j, False).start()
        return carry

    lax.fori_loop(0, owners - 1, start_out, 0)
    arrived_ref[me] = outbuf[me]

    chunk_rows = packed.shape[3]
    share = width // owners
    sections = wide + blocks
    per = -(-sections // groups)
    piece = share // groups
    sides = groups // 2

    def put(j, section, block):
        q, r = section // per, section % per
        packed[j, q // sides, q % sides, r * share : (r + 1) * share] = block.astype(BF16)

    if per * groups != sections or chunk_rows != per * share + piece:
        packed[...] = jnp.zeros_like(packed)
    for c in range(blocks):
        grad = matmul_tn(sw_s[:, lane(c)], dy_s[...])
        for n in range(LANES // share):
            for s in range(blocks):
                put(c * (LANES // share) + n, wide + s, grad[n * share : (n + 1) * share, lane(s)])

    back_ref[...] = sum_finish(1)
    bias_mean = row_of(back_ref, 0, blocks) / total_frames
    gain_mean = row_of(back_ref, blocks, blocks) / total_frames
    scale = bn_gain * bn_inverse
    xacc[...] = jnp.zeros_like(xacc)

    def backward(i, carry):
        rows = rows_of(i)
        lengths = lengths_of(i)
        grad_conv = scale * (fac_s[rows] - bias_mean - conv_s[rows] * gain_mean)
        grad_conv = keep_live(grad_conv, lengths, span).astype(BF16)
        spect = matmul(fwd_ref[...], grad_conv)
        saved = spect_s[spec_rows(i)]
        wr, wi, wn = wspec[:half], wspec[half : 2 * half], wspec[2 * half :]
        mixed, terms = [], [None] * 3
        for u in range(group):
            re = spect[u * size : u * size + half]
            im = spect[u * size + half : (u + 1) * size]
            sre = saved[u * size : u * size + half]
            sim = saved[u * size + half : (u + 1) * size]
            mixed.append((wr * re + wi * im).astype(BF16))
            mixed.append((wn * im - wi * re).astype(BF16))
            new = (re * sre, im * sim, re * sim - im * sre)
            terms = [b if a is None else a + b for a, b in zip(terms, new)]
        for n in range(3):
            xacc[n * half : (n + 1) * half] += terms[n]
        grad_gated = matmul(inv_ref[...], jnp.concatenate(mixed, axis=0))
        grad_gated = keep_live(grad_gated, lengths, span)
        gate = gate_s[rows]
        left = grad_gated * gate
        ga_s[rows, :width] = left.astype(BF16)
        ga_s[rows, width:] = (left * linear_s[rows] * (1.0 - gate)).astype(BF16)
        return carry

    lax.fori_loop(0, steps, backward, 0)
    grad_taps = matmul_exact(corr_ref[...], xacc[...])
    flat[...] = jnp.zeros_like(flat)
    for c in range(blocks):
        grad = matmul_tn(h_s[:, lane(c)], ga_s[...])
        flat[: taps + 1] = grad_taps[:, lane(c)]
        turned = flat[...].T.astype(BF16)
        for n in range(LANES // share):
            j = c * (LANES // share) + n
            for s in range(wide):
                put(j, s, grad[n * share : (n + 1) * share, lane(s)])
            for q in range(groups):
                packed[j, q // sides, q % sides, per * share : per * share + piece] = turned[
                    n * share + q * piece : n * share + (q + 1) * piece
                ]

    core, side = lax.rem(dp, 2), dp // 2
    partner = side * 2 + (1 - core)

    def remote(source, target, sems, i, j, device):
        return pltpu.make_async_remote_copy(
            src_ref=source,
            dst_ref=target,
            send_sem=sems.at[0, i],
            recv_sem=sems.at[1, j],
            device_id=device,
            device_id_type=MESH,
        )

    def bucket_of(i):
        return lax.rem(me + 1 + i, owners)

    def swap(i):
        bucket = bucket_of(i)
        return remote(packed.at[bucket, 1 - core], first.at[bucket], core_sems, i, i, (partner, me))

    def to_side(i, n, arriving):
        bucket = bucket_of(i)
        other = lax.rem(side + n, sides)
        slot = other if arriving else side
        return remote(
            first_sum.at[bucket, other], second.at[slot, bucket], pair_sems,
            n * owners + i, slot * owners + i, (other * 2 + core, me),
        )

    def to_owner(i, arriving):
        other = lax.rem(me + i, owners)
        slot = other if arriving else me
        return remote(second_sum.at[other], third.at[slot], row_sems, i, slot, (dp, other))

    def to_group(i, arriving):
        other = lax.rem(dp + i, groups)
        device = other if arriving else dp
        slot = lax.rem(device, 2) * sides + device // 2
        return remote(mine, reduced_ref.at[slot], all_sems, i, slot, (other, me))

    def start_swap(i, carry):
        swap(i).start()
        return carry

    def add_first(i, carry):
        bucket = bucket_of(i)
        swap(i).wait_recv()
        total = packed[bucket, core].astype(F32) + first[bucket].astype(F32)
        first_sum[bucket] = total.astype(BF16)
        for n in range(1, sides):
            to_side(i, n, False).start()
        return carry

    def add_second(i, carry):
        bucket = bucket_of(i)
        total = first_sum[bucket, side].astype(F32)
        for n in range(1, sides):
            to_side(i, n, True).wait_recv()
            total = total + second[lax.rem(side + n, sides), bucket].astype(F32)
        second_sum[bucket] = total.astype(BF16)
        return carry

    def add_and_send(i, carry):
        add_second(i, carry)
        to_owner(i + 1, False).start()
        return carry

    lax.fori_loop(0, owners, start_swap, 0)
    acc[...] = jnp.zeros_like(acc)

    def last(i, carry):
        rows = rows_of(i)
        lengths = lengths_of(i)
        grad_h = matmul_nt(ga_s[rows], w_in_ref[...])
        normed, inverse = normed_s[rows], inverse_s[rows][:, :1]
        acc[0] += fold_rows(grad_h * normed)
        scaled = grad_h * gain_ref[...]
        inner_mean = jnp.mean(scaled * normed, axis=1, keepdims=True)
        grad_x = inverse * (scaled - jnp.mean(scaled, axis=1, keepdims=True) - normed * inner_mean)
        grads_ref[rows] = keep_live(grad_x, lengths, span).astype(BF16)
        return carry

    lax.fori_loop(0, steps // 4, last, 0)
    lax.fori_loop(0, owners, add_first, 0)
    lax.fori_loop(steps // 4, steps // 2, last, 0)
    lax.fori_loop(0, owners - 1, add_and_send, 0)
    add_second(owners - 1, 0)
    third[me] = second_sum[me]
    lax.fori_loop(steps // 2, steps, last, 0)
    gather_parts(2)
    sum_start(2)

    def wait_owner(i, carry):
        to_owner(i, True).wait_recv()
        return carry

    lax.fori_loop(1, owners, wait_owner, 0)
    total = lax.fori_loop(
        1, owners, lambda i, t: t + third[i].astype(F32), third[0].astype(F32)
    )
    mine[...] = total.astype(BF16)

    def send_group(i, carry):
        to_group(i, False).start()
        return carry

    def wait_group(i, carry):
        to_group(i, True).wait_recv()
        return carry

    lax.fori_loop(1, groups, send_group, 0)
    reduced_ref[core * sides + side] = mine[...]
    ln_ref[...] = sum_finish(2)
    lax.fori_loop(1, groups, wait_group, 0)

    def finish_out(j, carry):
        out_copy(j, True).wait_recv()
        out_copy(j, False).wait_send()
        up_copy(j, 0, False).wait_send()
        up_copy(j, 1, False).wait_send()
        return carry

    lax.fori_loop(0, owners - 1, finish_out, 0)

    def finish_sums(i, carry):
        for n in range(3):
            sum_copy(n, i, rank).wait_send()
        return carry

    lax.fori_loop(1, count, finish_sums, 0)

    def finish_first(i, carry):
        swap(i).wait_send()
        for n in range(1, sides):
            to_side(i, n, False).wait_send()
        return carry

    def finish_owner(i, carry):
        to_owner(i, False).wait_send()
        return carry

    def finish_group(i, carry):
        to_group(i, False).wait_send()
        return carry

    lax.fori_loop(0, owners, finish_first, 0)
    lax.fori_loop(1, owners, finish_owner, 0)
    lax.fori_loop(1, groups, finish_group, 0)


def finish_kernel(
    taps, per, piece,
    meta, grads_ref, arrived_ref, reduced_ref, back_ref, ln_ref,
    out_ref, grad_frames_ref, win_ref, wout_ref, taps_ref, ln_out_ref, gain_ref, bias_ref,
    stage, flat, sems,
):
    me = lax.axis_index("bucket")
    slots, span, width = arrived_ref.shape
    own_rows = out_ref.shape[0]
    blocks = width // LANES
    share = win_ref.shape[0]
    wide = win_ref.shape[1] // LANES
    owners = width // share

    def row_copy(i):
        source = pl.ds(pl.multiple_of(i * span, PACK), span)
        target = pl.ds(pl.multiple_of(meta[1, i] * span, PACK), span)
        return pltpu.make_async_copy(
            grads_ref.at[source], grad_frames_ref.at[target], sems.at[i]
        )

    def start(i, carry):
        row_copy(i).start()
        return carry

    lax.fori_loop(0, slots, start, 0)

    def place(u, carry):
        begin = meta[2, u]
        for c in range(blocks):
            stage[c, pl.ds(begin, span)] = arrived_ref[u, :, lane(c)].astype(F32)
        return carry

    lax.fori_loop(0, slots, place, 0)

    def section(s):
        q, r = s // per, s % per
        return reduced_ref[q, r * share : (r + 1) * share].astype(F32)

    for c in range(blocks):
        out_ref[:, lane(c)] = stage[c, :own_rows].astype(BF16)
        wout_ref[:, lane(c)] = section(wide + c)
    for c in range(wide):
        win_ref[:, lane(c)] = section(c)
    flat[...] = jnp.zeros_like(flat)
    for q in range(reduced_ref.shape[0]):
        flat[q * piece : (q + 1) * piece] = reduced_ref[
            q, per * share : per * share + piece
        ].astype(F32)
    taps_ref[...] = flat[...].T[:taps, :share]
    row = jnp.zeros((1, share), F32)
    for j in range(owners):
        c, n = j * share // LANES, j * share % LANES
        row = jnp.where(me == j, ln_ref[c : c + 1, n : n + share], row)
    ln_out_ref[...] = row
    bias_ref[...] = row_of(back_ref, 0, blocks)
    gain_ref[...] = row_of(back_ref, blocks, blocks)

    def wait(i, carry):
        row_copy(i).wait()
        return carry

    lax.fori_loop(0, slots, wait, 0)


def in_hbm(array):
    return pltpu.with_memory_space_constraint(array, pltpu.HBM)


def local(frames, lengths, owner_ids, upstream, ln_gain, w_in, w_dw, bn_gain, bn_bias, w_out):
    groups, owners = lax.axis_size("dp"), lax.axis_size("bucket")
    all_rows, width = frames.shape
    taps = w_dw.shape[1]
    slots = lengths.shape[1] // owners
    span = all_rows // slots
    pairs = slots // owners
    own_rows = upstream.shape[0]
    blocks = width // LANES
    wide = w_in.shape[1] // LANES
    count = groups * owners
    total_frames = float(own_rows * count)
    in_vmem = pl.BlockSpec(memory_space=pltpu.VMEM)
    in_smem = pl.BlockSpec(memory_space=pltpu.SMEM)
    anywhere = pl.BlockSpec(memory_space=pl.ANY)
    group = pairs * max(1, 4 // pairs)
    size, fwd, inv, spec, corr = transform_tables(span, taps, group)
    chunk = pairs * span
    early = -(-chunk // 3 // PACK) * PACK
    share = width // owners
    per = -(-(wide + blocks) // groups)
    piece = share // groups
    chunk_rows = per * share + -(-piece // PACK) * PACK
    sides = groups // 2

    meta = pl.pallas_call(
        functools.partial(tables_kernel, slots),
        in_specs=[in_smem, in_smem],
        out_specs=in_smem,
        out_shape=jax.ShapeDtypeStruct((3, slots + SUB), jnp.int32),
        scratch_shapes=[pltpu.SMEM((owners,), jnp.int32)],
        name="tables",
    )(in_hbm(lengths), in_hbm(owner_ids))

    sums_shape = (2 * blocks, LANES)
    tall = pltpu.VMEM((all_rows, width), F32)
    short = pltpu.VMEM((all_rows, width), BF16)
    chunks = pltpu.VMEM((owners, chunk, width), BF16)
    rows_kind = (chunk_rows, LANES)
    grads, arrived, reduced, back, ln_total = pl.pallas_call(
        functools.partial(
            step_kernel, groups, owners, group, taps, size, early, total_frames
        ),
        in_specs=[in_smem] + [anywhere] * 4 + [in_vmem] * 8,
        out_specs=[in_vmem] * 5,
        out_shape=[
            jax.ShapeDtypeStruct((all_rows, width), BF16),
            jax.ShapeDtypeStruct((owners, chunk, width), BF16),
            jax.ShapeDtypeStruct((groups,) + rows_kind, BF16),
            jax.ShapeDtypeStruct(sums_shape, F32),
            jax.ShapeDtypeStruct(sums_shape, F32),
        ],
        scratch_shapes=[
            pltpu.VMEM((slots, span, width), BF16),
            pltpu.VMEM((own_rows, width), BF16),
            pltpu.VMEM(w_in.shape, BF16),
            pltpu.VMEM(w_out.shape, BF16),
            pltpu.VMEM((blocks, own_rows + span, LANES), F32),
            chunks,
            chunks,
            chunks,
            tall,
            pltpu.VMEM((all_rows, LANES), F32),
            tall,
            tall,
            short,
            pltpu.VMEM((slots * size, width), F32),
            tall,
            tall,
            short,
            short,
            pltpu.VMEM((all_rows, w_in.shape[1]), BF16),
            pltpu.VMEM((3 * size // 2, width), F32),
            pltpu.VMEM((2, SUB, width), F32),
            pltpu.VMEM((3 * size // 2, width), F32),
            pltpu.VMEM(sums_shape, F32),
            pltpu.VMEM((3,) + sums_shape, F32),
            pltpu.VMEM((3, count) + sums_shape, F32),
            pltpu.VMEM((LANES, LANES), F32),
            pltpu.VMEM((owners, 2, sides) + rows_kind, BF16),
            pltpu.VMEM((owners, sides) + rows_kind, BF16),
            pltpu.VMEM((owners, sides) + rows_kind, BF16),
            pltpu.VMEM((sides, owners) + rows_kind, BF16),
            pltpu.VMEM((owners,) + rows_kind, BF16),
            pltpu.VMEM((owners,) + rows_kind, BF16),
            pltpu.VMEM(rows_kind, BF16),
            pltpu.SemaphoreType.DMA((4,)),
            pltpu.SemaphoreType.DMA((3, count)),
            pltpu.SemaphoreType.DMA((3, count)),
            pltpu.SemaphoreType.DMA((2, owners)),
            pltpu.SemaphoreType.DMA((2, owners)),
            pltpu.SemaphoreType.DMA((owners,)),
            pltpu.SemaphoreType.DMA((owners,)),
            pltpu.SemaphoreType.DMA((2, owners)),
            pltpu.SemaphoreType.DMA((2, sides * owners)),
            pltpu.SemaphoreType.DMA((2, owners)),
            pltpu.SemaphoreType.DMA((2, groups)),
        ],
        compiler_params=pltpu.CompilerParams(
            collective_id=0, has_side_effects=True, vmem_limit_bytes=54 << 20
        ),
        cost_estimate=pl.CostEstimate(
            flops=10**10, bytes_accessed=4 * 10**7, transcendentals=0
        ),
        name="step",
    )(
        meta, *map(in_hbm, (frames.reshape(slots, span, width), upstream, w_in, w_out)),
        ln_gain[None], bn_gain[None], bn_bias[None], jnp.pad(w_dw.T, ((0, 1), (0, 0))),
        fwd, inv, spec, corr,
    )

    row_shape = jax.ShapeDtypeStruct((1, width), F32)
    out_frames, grad_frames, grad_win, grad_wo, grad_taps, grad_ln, grad_gain, grad_bias = (
        pl.pallas_call(
            functools.partial(finish_kernel, taps, per, piece),
            in_specs=[in_smem] + [in_vmem] * 5,
            out_specs=[in_vmem, anywhere] + [in_vmem] * 6,
            out_shape=[
                jax.ShapeDtypeStruct((own_rows, width), BF16),
                jax.ShapeDtypeStruct((all_rows, width), BF16),
                jax.ShapeDtypeStruct((share, w_in.shape[1]), F32),
                jax.ShapeDtypeStruct((share, width), F32),
                jax.ShapeDtypeStruct((taps, share), F32),
                jax.ShapeDtypeStruct((1, share), F32),
                row_shape,
                row_shape,
            ],
            scratch_shapes=[
                pltpu.VMEM((blocks, own_rows + span, LANES), F32),
                pltpu.VMEM((LANES, LANES), F32),
                pltpu.SemaphoreType.DMA((slots,)),
            ],
            compiler_params=pltpu.CompilerParams(vmem_limit_bytes=24 << 20),
            name="finish",
        )(meta, grads, arrived.reshape(slots, span, width), reduced, back, ln_total)
    )
    return (
        out_frames,
        grad_frames,
        grad_win,
        grad_wo,
        grad_taps.T,
        grad_ln[0],
        grad_gain[0],
        grad_bias[0],
    )


def solution(mesh):
    placed = (
        P(("dp", "bucket"), None),
        P("dp", None),
        P("dp", None),
        P(("dp", "bucket"), None),
        P(),
        P(),
        P(),
        P(),
        P(),
        P(),
    )
    return jax.shard_map(
        local,
        mesh=mesh,
        in_specs=placed,
        out_specs=(
            P(("dp", "bucket"), None),
            P(("dp", "bucket"), None),
            P("bucket", None),
            P("bucket", None),
            P("bucket", None),
            P("bucket"),
            P(),
            P(),
        ),
        check_vma=False,
    )
```

time: 136 us -> 116 us (0.85)
  starting transfers between devices: 11.2 us -> 0 us
  Pallas kernels: 119 us -> 108 us
  local copies, waits for them, and re-layouts: 4.26 us -> 6.59 us
    all_to_all x2 -> x0, starting transfers between devices: 11.2 us -> none  [exchange(): lax.all_to_all(slots, 'bucket', split_axis=0, concat_axis=0, tiled=True)]
    pallas_call x8 -> x3, Pallas kernels: 119 us -> 108 us  [the longest x1 102 us: local(): pl.pallas_call(functools.partial(step_kernel, groups, owners, group, taps...]
    unnamed x17 -> x12, local copies, waits for them, and re-layouts: 2.97 us -> 5.11 us
    pad x1, local copies, waits for them, and re-layouts: 0.01 us -> 1.48 us  [local(): jnp.pad(w_dw.T, ((0, 1), (0, 0)))]
  transfers between devices with their start and end apart: 2 -> 0, of which waited for: 0 -> 0; matrix products, arithmetic and copies ran while one was open for 0% -> 0% of each run, Pallas kernels for 69% -> 0%
where the time goes in v1:
time: 116 us; the launch traced here: 115 us
  Pallas kernels  108 us (93%)
  local copies, waits for them, and re-layouts  6.59 us (6%)
    pallas_call x1, Pallas kernels, local(): pl.pallas_call(functools.partial(step_kernel, groups, owners, group, taps...  102 us
    unnamed x12, local copies, waits for them, and re-layouts  5.11 us
    pallas_call x1, Pallas kernels, local(): pl.pallas_call(functools.partial(finish_kernel, taps, per, piece), in_spe...  3.36 us
    pallas_call x1, Pallas kernels, local(): pl.pallas_call(functools.partial(tables_kernel, slots), in_specs=[in_smem...  3.07 us

profile of v1, /device:TPU:0, one launch (start us, length us, event | category | flops | bytes accessed | tf_op | source)
XLA Modules:
  0.0 115.5 jit_solution(6881963666204049234)
XLA Ops:
  0.6 3.1 %tables.1.meta = s32[3,40]{1,0:T(4,128)} custom-call(s32[1,256]{1,0:T(1,128)} %lens_ref.1, s32[1,256]{1,0:T(1,128)} %owners_ref.1), custom_call_target="tpu_custom_call" | custom-call | tf_op jit(solution)/shard_map/tables/pallas_call | solution.py:697
  3.7 1.5 %pad.4.w_taps_ref = f32[32,512]{1,0:T(8,128)} pad(f32[31,512]{1,0:T(8,128)} %bitcast.11, f32[]{:T(128)} %constant.10.clone.1), padding=0_1x0_0 | pad | bytes 129028 | tf_op jit(solution)/shard_map/jit(_pad)/pad | solution.py:779
  5.2 0.0 copy-start.3
  5.2 101.8 %step.1 = (bf16[1536,512]{1,0:T(8,128)(2,1)}, bf16[8,192,512]{2,1,0:T(8,128)(2,1)}, bf16[4,208,128]{2,1,0:T(8,128)(2,1)}, f32[8,128]{1,0:T(8,128)}, f32[8,128]{1,0:T(8,128)}) custom-call(s32[3,40]{1,0:T(4,128)} %tables.1.meta, bf16[32,48,512]{2,1,0:T(8,128)(2,1)} %bitcast.12, bf16[768,512]{1,0:T(8,128)(2,1)} %up_hbm.1, bf16[512,1024]{1,0:T(8,128)(2,1)} %w_in_hbm.1, ...), custom_call_target="tpu_custom_call" | custom-call | flops 10000000000 | bytes 40000000 | tf_op jit(solution)/shard_map/step/pallas_call | solution.py:711
  107.0 0.0 copy-done.3
  107.0 0.0 copy-start
  107.0 1.4 %copy-done = bf16[1536,512]{1,0:T(8,128)(2,1)S(1)} copy-done((bf16[1536,512]{1,0:T(8,128)(2,1)S(1)}, bf16[1536,512]{1,0:T(8,128)(2,1)}, u32[]{:S(2)}) %copy-start) | copy-done | bytes 1572888
  108.4 0.0 copy-start.1
  108.4 1.4 %copy-done.1 = bf16[8,192,512]{2,1,0:T(8,128)(2,1)S(1)} copy-done((bf16[8,192,512]{2,1,0:T(8,128)(2,1)S(1)}, bf16[8,192,512]{2,1,0:T(8,128)(2,1)}, u32[]{:S(2)}) %copy-start.1) | copy-done | bytes 1572888
  109.8 0.0 copy-start.2
  109.8 0.9 copy-done.2
  110.7 0.0 copy-start.4
  110.7 0.7 copy-done.4
  111.4 0.0 copy-start.5
  111.4 0.7 copy-done.5
  112.1 3.4 %finish.1 = (bf16[768,512]{1,0:T(8,128)(2,1)}, bf16[1536,512]{1,0:T(8,128)(2,1)}, f32[64,1024]{1,0:T(8,128)}, f32[64,512]{1,0:T(8,128)}, f32[31,64]{1,0:T(8,128)...) custom-call(s32[3,40]{1,0:T(4,128)S(1)} %copy-done.3, bf16[1536,512]{1,0:T(8,128)(2,1)S(1)} %copy-done, ...), custom_call_target="tpu_custom_call" | custom-call | tf_op jit(solution)/shard_map/finish/pallas_call | solution.py:785
Async XLA Ops:
  5.2 101.8 %copy-start.3 = (s32[3,40]{1,0:T(4,128)S(1)}, s32[3,40]{1,0:T(4,128)}, u32[]{:S(2)}) copy-start(s32[3,40]{1,0:T(4,128)} %tables.1.meta) | copy-start | bytes 1444
  107.0 1.4 %copy-start = (bf16[1536,512]{1,0:T(8,128)(2,1)S(1)}, bf16[1536,512]{1,0:T(8,128)(2,1)}, u32[]{:S(2)}) copy-start(bf16[1536,512]{1,0:T(8,128)(2,1)} %get-tuple-element.21.grads_ref) | copy-start | bytes 4718596
  108.4 1.4 %copy-start.1 = (bf16[8,192,512]{2,1,0:T(8,128)(2,1)S(1)}, bf16[8,192,512]{2,1,0:T(8,128)(2,1)}, u32[]{:S(2)}) copy-start(bf16[8,192,512]{2,1,0:T(8,128)(2,1)} %get-tuple-element.22) | copy-start | bytes 4718596
  109.8 0.9 copy-start.2
  110.7 0.7 copy-start.4
  111.4 0.7 copy-start.5

commit v2 on v1

v2 whole, which is shorter than its diff:
```python
import functools

import jax
import jax.numpy as jnp
import numpy as np
from jax import lax
from jax.experimental import pallas as pl
from jax.experimental.pallas import tpu as pltpu
from jax.sharding import PartitionSpec as P

EPSILON = 1e-05
LANES = 128
SUB = 8
PACK = 16
STEP_VMEM = 50 << 20
MESH = pl.DeviceIdType.MESH
BF16 = jnp.bfloat16
F32 = jnp.float32


def lane(c):
    return slice(c * LANES, (c + 1) * LANES)


def row_of(packed, first, blocks):
    return jnp.concatenate([packed[first + c : first + c + 1] for c in range(blocks)], axis=1)


def keep_live(values, lengths, span):
    position = lax.broadcasted_iota(jnp.int32, (span, values.shape[1]), 0)
    parts = [
        jnp.where(position < length, values[i * span : (i + 1) * span], 0.0)
        for i, length in enumerate(lengths)
    ]
    return jnp.concatenate(parts, axis=0)


def fold_rows(values):
    rows, width = values.shape
    return jnp.sum(values.reshape(rows // SUB, SUB, width), axis=0)


def matmul(a, b):
    return jnp.dot(a, b, preferred_element_type=F32)


def matmul_nt(a, b):
    return lax.dot_general(a, b, (((1,), (1,)), ((), ())), preferred_element_type=F32)


def matmul_tn(a, b):
    return lax.dot_general(a, b, (((0,), (0,)), ((), ())), preferred_element_type=F32)


def matmul_exact(a, b):
    return jnp.dot(a, b, preferred_element_type=F32, precision=lax.Precision.HIGHEST)


def transform_tables(span, taps, group):
    size = -(-(span + taps // 2) // (2 * PACK)) * (2 * PACK)
    half = size // 2
    freq = np.arange(half)[:, None]

    def angle(times):
        return 2.0 * np.pi * freq * np.asarray(times)[None, :] / size

    def flip(times):
        return np.where(np.asarray(times) % 2 == 0, 1.0, -1.0)

    times = np.arange(span)
    real, imag = np.cos(angle(times)), -np.sin(angle(times))
    imag[0] = flip(times)
    forward = np.concatenate([real, imag], axis=0)
    scale = np.where(np.arange(size) % half == 0, 1.0, 2.0) / size
    inverse = (forward * scale[:, None]).T
    lags = taps // 2 - np.arange(taps)
    wr, wi, wn = np.cos(angle(lags)), -np.sin(angle(lags)), np.cos(angle(lags))
    wi[0] = 0.0
    wn[0] = flip(lags)
    spectrum = np.concatenate([wr, wi, wn], axis=0)
    spectrum = np.pad(spectrum, ((0, 0), (0, 1)))
    back = -lags
    cr, cn, ci = np.cos(angle(back)), np.cos(angle(back)), -np.sin(angle(back))
    cn[0] = flip(back)
    ci[0] = 0.0
    both = np.concatenate([scale[:half], scale[half:], scale[half:]])
    correlate = (np.concatenate([cr, cn, ci], axis=0) * both[:, None]).T
    correlate = np.pad(correlate, ((0, 1), (0, 0)))
    eye = np.eye(group)
    return (
        size,
        jnp.asarray(np.kron(eye, forward), BF16),
        jnp.asarray(np.kron(eye, inverse), BF16),
        jnp.asarray(spectrum, F32),
        jnp.asarray(correlate, F32),
    )


def chunk_bounds(own_rows, pairs, span, loaders):
    rows = [min(pairs * span, (own_rows - b * pairs) // (loaders - b)) for b in range(loaders)]
    return [-(-r // PACK) * PACK for r in rows]


def tables_kernel(slots, lens_ref, owners_ref, meta_ref, counts):
    me = lax.axis_index("bucket")
    loaders = lens_ref.shape[1] // slots
    pairs = slots // loaders

    def look(b, start):
        meta_ref[2, b] = start
        for j in range(slots):
            at = b * slots + j
            start = start + jnp.where(owners_ref[0, at] == me, lens_ref[0, at], 0)
        return start

    lax.fori_loop(0, loaders, look, jnp.int32(0))

    def clear(i, carry):
        counts[i] = 0
        return carry

    lax.fori_loop(0, loaders, clear, 0)

    def place(i, carry):
        owner = owners_ref[0, me * slots + i]
        rank = counts[owner]
        counts[owner] = rank + 1
        at = owner * pairs + rank
        meta_ref[0, at] = lens_ref[0, me * slots + i]
        meta_ref[1, at] = i
        return carry

    lax.fori_loop(0, slots, place, 0)


def reducer(groups, owners, dp, me, src, out, refs):
    first, first_sum, second, second_sum, twin, twin_sum, third, mine = refs[:8]
    core_sems, pair_sems, twin_sems, row_sems, all_sems = refs[8:]
    sides = groups // 2
    core, side = lax.rem(dp, 2), dp // 2
    partner = side * 2 + (1 - core)

    def remote(source, target, sems, i, j, device):
        return pltpu.make_async_remote_copy(
            src_ref=source,
            dst_ref=target,
            send_sem=sems.at[0, i],
            recv_sem=sems.at[1, j],
            device_id=device,
            device_id_type=MESH,
        )

    def bucket_of(i):
        return lax.rem(me + 1 + i, owners)

    def swap(i):
        bucket = bucket_of(i)
        return remote(src.at[bucket, 1 - core], first.at[bucket], core_sems, i, i, (partner, me))

    def to_side(i, n, arriving):
        bucket = bucket_of(i)
        other = lax.rem(side + n, sides)
        slot = other if arriving else side
        return remote(
            first_sum.at[bucket, other], second.at[slot, bucket], pair_sems,
            n * owners + i, slot * owners + i, (other * 2 + core, me),
        )

    near = lax.rem(me, 2)
    mate = me + 1 - 2 * near
    pairs = owners // 2

    def pair_of(i):
        return lax.rem(me // 2 + 1 + i, pairs)

    def to_mate(i):
        pair = pair_of(i)
        return remote(second_sum.at[pair * 2 + 1 - near], twin.at[pair], twin_sems, i, i, (dp, mate))

    def to_owner(i, arriving):
        pair = lax.rem(me // 2 + i, pairs)
        slot = pair if arriving else me // 2
        return remote(
            twin_sum.at[pair], third.at[slot], row_sems, i, slot, (dp, pair * 2 + near)
        )

    def to_group(i, arriving):
        other = lax.rem(dp + i, groups)
        device = other if arriving else dp
        slot = lax.rem(device, 2) * sides + device // 2
        return remote(mine, out.at[slot], all_sems, i, slot, (other, me))

    def loop(low, high, body):
        def step(i, carry):
            body(i)
            return carry

        lax.fori_loop(low, high, step, 0)

    def add_first(i):
        bucket = bucket_of(i)
        swap(i).wait_recv()
        total = src[bucket, core].astype(F32) + first[bucket].astype(F32)
        first_sum[bucket] = total.astype(BF16)
        for n in range(1, sides):
            to_side(i, n, False).start()

    def add_second(i):
        bucket = bucket_of(i)
        total = first_sum[bucket, side].astype(F32)
        for n in range(1, sides):
            to_side(i, n, True).wait_recv()
            total = total + second[lax.rem(side + n, sides), bucket].astype(F32)
        second_sum[bucket] = total.astype(BF16)

    def add_twin(i):
        pair = pair_of(i)
        to_mate(i).wait_recv()
        total = second_sum[pair * 2 + near].astype(F32) + twin[pair].astype(F32)
        twin_sum[pair] = total.astype(BF16)

    def twin_and_send(i):
        add_twin(i)
        to_owner(i + 1, False).start()

    def stage_swap():
        loop(0, owners, lambda i: swap(i).start())

    def stage_side():
        loop(0, owners, add_first)

    def stage_mate():
        loop(0, owners, add_second)
        loop(0, pairs, lambda i: to_mate(i).start())

    def stage_owner():
        loop(0, pairs - 1, twin_and_send)
        add_twin(pairs - 1)
        third[me // 2] = twin_sum[me // 2]

    def stage_group():
        loop(1, pairs, lambda i: to_owner(i, True).wait_recv())
        total = lax.fori_loop(
            1, pairs, lambda i, t: t + third[i].astype(F32), third[0].astype(F32)
        )
        mine[...] = total.astype(BF16)
        loop(1, groups, lambda i: to_group(i, False).start())
        out[core * sides + side] = mine[...]

    def stage_end():
        loop(1, groups, lambda i: to_group(i, True).wait_recv())

        def first_sent(i):
            swap(i).wait_send()
            for n in range(1, sides):
                to_side(i, n, False).wait_send()

        loop(0, owners, first_sent)
        loop(0, pairs, lambda i: to_mate(i).wait_send())
        loop(1, pairs, lambda i: to_owner(i, False).wait_send())
        loop(1, groups, lambda i: to_group(i, False).wait_send())

    return stage_swap, stage_side, stage_mate, stage_owner, stage_group, stage_end


def step_kernel(
    groups, owners, group, taps, size, early, early_out, late_out, bounds, total_frames,
    meta, *refs,
):
    sources, refs = refs[:12], refs[12:]
    grads_ref, arrived_ref, reduced_ref, reduced_out_ref, back_ref, ln_ref = refs[:6]
    targets, refs = refs[6:18], refs[18:]
    up, w_dw_ref, spec_ref, frames, w_in_ref, gain_ref, fwd_ref, inv_ref = targets[:8]
    w_out_ref, bn_gain_ref, bn_bias_ref, corr_ref = targets[8:]
    (
    stage, outgoing, arrive, outbuf,
    normed_s, inverse_s, linear_s, gate_s, h_s, spect_s, conv_s, fac_s, sw_s, dy_s, ga_s,
    w_taps, wspec, acc, xacc, tot, parts, mids, slots_a, slots_b, flat,
    packed, packed_out, local_sems, up_send, up_recv, out_send, out_recv,
    a_send, a_recv, b_send, b_recv, *reduce_refs,
    ) = refs
    dp, me = lax.axis_index("dp"), lax.axis_index("bucket")
    slot_count, span, width = frames.shape
    all_rows = slot_count * span
    own_rows = up.shape[0]
    blocks = width // LANES
    wide = w_in_ref.shape[1] // LANES
    chunk = all_rows // owners
    pairs = slot_count // owners
    steps = slot_count // group
    held = group // pairs
    grows = group * span
    half = size // 2
    far = owners // 2
    barrier = pltpu.get_barrier_semaphore()

    def loop(low, high, body):
        def step(i, carry):
            body(i)
            return carry

        lax.fori_loop(low, high, step, 0)

    def peer_of(m):
        bits = range((owners - 1).bit_length())
        return sum(lax.rem(me // 2**k + m // 2**k, 2) * 2**k for k in bits)

    def greet_group(i):
        pl.semaphore_signal(
            barrier, inc=1, device_id=(lax.rem(dp + i, groups), me), device_id_type=MESH
        )

    def greet_owner(m):
        pl.semaphore_signal(barrier, inc=1, device_id=(dp, peer_of(m)), device_id_type=MESH)

    loop(1, groups, greet_group)
    loop(1, owners, greet_owner)
    loads = [
        pltpu.make_async_copy(source, target, local_sems.at[n])
        for n, (source, target) in enumerate(zip(sources, targets))
    ]
    for load in loads:
        load.start()

    loads[0].wait()
    for c in range(blocks):
        stage[c, :own_rows] = up[:, lane(c)].astype(F32)
        stage[c, own_rows:] = jnp.zeros((chunk, LANES), F32)

    def lay_out(b):
        start = meta[2, b]
        for c in range(blocks):
            outgoing[b, :, lane(c)] = stage[c, pl.ds(start, chunk)].astype(BF16)

    loop(0, owners, lay_out)
    arrive[me] = outgoing[me]

    def sized(index, body):
        for rows in sorted(set(bounds)):
            low = bounds.index(rows)
            high = low + bounds.count(rows)

            @pl.when(jnp.logical_and(index >= low, index < high))
            def _():
                body(rows)

    def up_copy(m, part, rows, arriving):
        peer = peer_of(m)
        slot = peer if arriving else me
        span_of = pl.ds(0, early) if part == 0 else pl.ds(early, rows - early)
        return pltpu.make_async_remote_copy(
            src_ref=outgoing.at[peer, span_of],
            dst_ref=arrive.at[slot, span_of],
            send_sem=up_send.at[part, m],
            recv_sem=up_recv.at[part, m],
            device_id=(dp, peer),
            device_id_type=MESH,
        )

    cuts = (0, early_out, late_out, chunk)

    def out_copy(m, part, rows, arriving):
        peer = peer_of(m)
        slot = peer if arriving else me
        low, high = cuts[part], min(cuts[part + 1], rows)
        return pltpu.make_async_remote_copy(
            src_ref=outbuf.at[peer, pl.ds(low, high - low)],
            dst_ref=arrived_ref.at[slot, pl.ds(low, high - low)],
            send_sem=out_send.at[part, m],
            recv_sem=out_recv.at[part, m],
            device_id=(dp, peer),
            device_id_type=MESH,
        )

    def each_out(loader, m, part, arriving, use):
        def body(rows):
            if rows > cuts[part]:
                use(out_copy(m, part, rows, arriving))

        sized(loader, body)

    def start_out(low, high, part):
        loop(
            low,
            high,
            lambda j: each_out(me, owners - 1 - j, part, False, lambda copy: copy.start()),
        )

    def start_up(part):
        def body(j):
            m = owners - 1 - j
            if part == 0:
                up_copy(m, 0, None, False).start()
            else:
                sized(peer_of(m), lambda rows: up_copy(m, 1, rows, False).start())

        loop(0, owners - 1, body)

    def a_copy(n, i, arriving):
        other = lax.rem(dp + i, groups)
        slot = lax.rem(dp + groups - i, groups) if arriving else dp
        return pltpu.make_async_remote_copy(
            src_ref=parts.at[n],
            dst_ref=slots_a.at[n, slot],
            send_sem=a_send.at[n, i],
            recv_sem=a_recv.at[n, i],
            device_id=(other, me),
            device_id_type=MESH,
        )

    def b_copy(n, m, arriving):
        peer = peer_of(m)
        slot = peer if arriving else me
        return pltpu.make_async_remote_copy(
            src_ref=mids.at[n],
            dst_ref=slots_b.at[n, slot],
            send_sem=b_send.at[n, m],
            recv_sem=b_recv.at[n, m],
            device_id=(dp, peer),
            device_id_type=MESH,
        )

    def sum_start(n):
        for k in range(2):
            row = jnp.sum(acc[k], axis=0, keepdims=True)
            for c in range(blocks):
                parts[n, k * blocks + c : k * blocks + c + 1] = row[:, lane(c)]
        loop(1, groups, lambda i: a_copy(n, i, False).start())
        slots_a[n, dp] = parts[n]

    def sum_middle(n):
        loop(1, groups, lambda i: a_copy(n, i, True).wait_recv())
        mids[n] = lax.fori_loop(1, groups, lambda i, t: t + slots_a[n, i], slots_a[n, 0])
        loop(0, owners - 1, lambda j: b_copy(n, owners - 1 - j, False).start())
        slots_b[n, me] = mids[n]

    def sum_finish(n):
        loop(1, owners, lambda m: b_copy(n, m, True).wait_recv())
        return lax.fori_loop(1, owners, lambda i, t: t + slots_b[n, i], slots_b[n, 0])

    loads[1].wait()
    loads[2].wait()
    w_taps[...] = jnp.zeros_like(w_taps)
    w_taps[:taps] = w_dw_ref[...]
    wspec[...] = matmul_exact(spec_ref[...], w_taps[...])
    acc[...] = jnp.zeros_like(acc)
    pl.semaphore_wait(barrier, groups + owners - 2)
    start_up(0)
    for load in loads[3:8]:
        load.wait()

    def rows_of(i):
        return pl.ds(pl.multiple_of(i * grows, PACK), grows)

    def spec_rows(i):
        return pl.ds(pl.multiple_of(i * group * size, PACK), group * size)

    def lengths_of(i):
        return [meta[0, i * group + u] for u in range(group)]

    def packing(lengths):
        column = lax.broadcasted_iota(jnp.int32, (1, grows), 1)
        target = jnp.full((1, grows), -1, jnp.int32)
        for u in range(group):
            first = (u // pairs) * chunk + sum(lengths[u - u % pairs : u], jnp.int32(0))
            at = column - u * span
            live = jnp.logical_and(at >= 0, at < lengths[u])
            target = jnp.where(live, at + first, target)
        row = lax.broadcasted_iota(jnp.int32, (grows, grows), 0)
        return jnp.where(row == target, 1.0, 0.0).astype(BF16)

    def forward(i):
        rows = rows_of(i)
        lengths = lengths_of(i)
        values = jnp.concatenate(
            [frames[meta[1, i * group + u]] for u in range(group)], axis=0
        ).astype(F32)
        centred = values - jnp.mean(values, axis=1, keepdims=True)
        inverse = lax.rsqrt(jnp.mean(centred * centred, axis=1, keepdims=True) + EPSILON)
        normed = centred * inverse
        h = (normed * gain_ref[...]).astype(BF16)
        projected = matmul(h, w_in_ref[...])
        linear, gate = projected[:, :width], jax.nn.sigmoid(projected[:, width:])
        normed_s[rows] = normed
        inverse_s[rows] = jnp.broadcast_to(inverse, (grows, LANES))
        linear_s[rows] = linear
        gate_s[rows] = gate
        h_s[rows] = h
        gated = keep_live(linear * gate, lengths, span).astype(BF16)
        spect = matmul(fwd_ref[...], gated)
        spect_s[spec_rows(i)] = spect
        wr, wi, wn = wspec[:half], wspec[half : 2 * half], wspec[2 * half :]
        mixed = []
        for u in range(group):
            re = spect[u * size : u * size + half]
            im = spect[u * size + half : (u + 1) * size]
            mixed.append((wr * re - wi * im).astype(BF16))
            mixed.append((wn * im + wi * re).astype(BF16))
        conv = matmul(inv_ref[...], jnp.concatenate(mixed, axis=0))
        conv_s[rows] = conv
        masked = keep_live(conv, lengths, span)
        acc[0] += fold_rows(masked)
        acc[1] += fold_rows(masked * masked)

    loop(0, steps, forward)
    sum_start(0)
    sum_middle(0)
    for load in loads[8:]:
        load.wait()
    tot[...] = sum_finish(0)
    start_up(1)
    centre = row_of(tot, 0, blocks) / total_frames
    variance = row_of(tot, blocks, blocks) / total_frames - centre * centre
    bn_inverse = lax.rsqrt(variance + EPSILON)
    acc[...] = jnp.zeros_like(acc)
    bn_gain, bn_bias = bn_gain_ref[...], bn_bias_ref[...]

    def swish(i):
        rows = rows_of(i)
        bn_normed = (conv_s[rows] - centre) * bn_inverse
        conv_s[rows] = bn_normed
        bn = bn_normed * bn_gain + bn_bias
        sig = jax.nn.sigmoid(bn)
        swished = (bn * sig).astype(BF16)
        sw_s[rows] = swished
        fac_s[rows] = sig * (1.0 + bn * (1.0 - sig))
        out = matmul(swished, w_out_ref[...]).astype(BF16)
        out = matmul(packing(lengths_of(i)), out).astype(BF16)
        for r in range(held):
            outbuf[i * held + r] = out[r * chunk : (r + 1) * chunk]

    loop(0, steps, swish)

    @pl.when(me >= far)
    def _():
        start_out(0, far, 0)

    def middle(t):
        m = lax.rem(owners - t * held, owners)
        i = peer_of(m) // held
        rows = rows_of(i)
        lengths = lengths_of(i)
        for r in range(held):
            owner = i * held + r
            bits = range((owners - 1).bit_length())
            gap = sum(lax.rem(me // 2**k + owner // 2**k, 2) * 2**k for k in bits)

            @pl.when(owner != me)
            def _():
                up_copy(gap, 0, None, True).wait_recv()
                sized(me, lambda rows: up_copy(gap, 1, rows, True).wait_recv())

        pieces = []
        position = lax.broadcasted_iota(jnp.int32, (chunk, width), 0)
        for r in range(held):
            total = sum(lengths[r * pairs : (r + 1) * pairs], jnp.int32(0))
            came = arrive[i * held + r].astype(F32)
            pieces.append(jnp.where(position < total, came, 0.0).astype(BF16))
        dy = matmul_tn(packing(lengths), jnp.concatenate(pieces, axis=0)).astype(BF16)
        dy_s[rows] = dy
        grad_bn = matmul_nt(dy, w_out_ref[...]) * fac_s[rows]
        fac_s[rows] = grad_bn
        acc[0] += fold_rows(grad_bn)
        acc[1] += fold_rows(grad_bn * conv_s[rows])

    loop(0, steps, middle)
    sum_start(1)
    sum_middle(1)

    arrived_ref[me] = outbuf[me]

    share = width // owners
    per, per_out = -(-wide // groups), -(-blocks // groups)
    piece = share // groups
    sides = groups // 2
    in_stages = reducer(groups, owners, dp, me, packed, reduced_ref, reduce_refs[:13])
    out_stages = reducer(groups, owners, dp, me, packed_out, reduced_out_ref, reduce_refs[13:])

    def put(target, count, j, section, block):
        q, r = section // count, section % count
        target[j, q // sides, q % sides, r * share : (r + 1) * share] = block.astype(BF16)

    if per_out * groups != blocks:
        packed_out[...] = jnp.zeros_like(packed_out)
    if per * groups != wide or packed.shape[3] != per * share + piece:
        packed[...] = jnp.zeros_like(packed)
    for c in range(blocks):
        grad = matmul_tn(sw_s[:, lane(c)], dy_s[...])
        for n in range(LANES // share):
            j = c * (LANES // share) + n
            for s in range(blocks):
                put(packed_out, per_out, j, s, grad[n * share : (n + 1) * share, lane(s)])
    out_stages[0]()
    back_ref[...] = sum_finish(1)

    @pl.when(me < far)
    def _():
        start_out(0, far, 0)

    start_out(0, far, 1)
    start_out(far, owners - 1, 0)
    start_out(far, owners - 1, 1)
    bias_mean = row_of(back_ref, 0, blocks) / total_frames
    gain_mean = row_of(back_ref, blocks, blocks) / total_frames
    scale = bn_gain * bn_inverse
    xacc[...] = jnp.zeros_like(xacc)

    def backward(i):
        rows = rows_of(i)
        lengths = lengths_of(i)
        grad_conv = scale * (fac_s[rows] - bias_mean - conv_s[rows] * gain_mean)
        grad_conv = keep_live(grad_conv, lengths, span).astype(BF16)
        spect = matmul(fwd_ref[...], grad_conv)
        saved = spect_s[spec_rows(i)]
        wr, wi, wn = wspec[:half], wspec[half : 2 * half], wspec[2 * half :]
        mixed, terms = [], [None] * 3
        for u in range(group):
            re = spect[u * size : u * size + half]
            im = spect[u * size + half : (u + 1) * size]
            sre = saved[u * size : u * size + half]
            sim = saved[u * size + half : (u + 1) * size]
            mixed.append((wr * re + wi * im).astype(BF16))
            mixed.append((wn * im - wi * re).astype(BF16))
            new = (re * sre, im * sim, re * sim - im * sre)
            terms = [b if a is None else a + b for a, b in zip(terms, new)]
        for n in range(3):
            xacc[n * half : (n + 1) * half] += terms[n]
        grad_gated = matmul(inv_ref[...], jnp.concatenate(mixed, axis=0))
        grad_gated = keep_live(grad_gated, lengths, span)
        gate = gate_s[rows]
        left = grad_gated * gate
        ga_s[rows, :width] = left.astype(BF16)
        ga_s[rows, width:] = (left * linear_s[rows] * (1.0 - gate)).astype(BF16)

    loop(0, steps // 2, backward)
    out_stages[1]()
    loop(steps // 2, steps, backward)
    out_stages[2]()
    grad_taps = matmul_exact(corr_ref[...], xacc[...])
    flat[...] = jnp.zeros_like(flat)
    for c in range(blocks):
        grad = matmul_tn(h_s[:, lane(c)], ga_s[...])
        flat[: taps + 1] = grad_taps[:, lane(c)]
        turned = flat[...].T.astype(BF16)
        for n in range(LANES // share):
            j = c * (LANES // share) + n
            for s in range(wide):
                put(packed, per, j, s, grad[n * share : (n + 1) * share, lane(s)])
            for q in range(groups):
                packed[j, q // sides, q % sides, per * share : per * share + piece] = turned[
                    n * share + q * piece : n * share + (q + 1) * piece
                ]
    in_stages[0]()
    acc[...] = jnp.zeros_like(acc)

    def last(i):
        rows = rows_of(i)
        lengths = lengths_of(i)
        grad_h = matmul_nt(ga_s[rows], w_in_ref[...])
        normed, inverse = normed_s[rows], inverse_s[rows][:, :1]
        acc[0] += fold_rows(grad_h * normed)
        scaled = grad_h * gain_ref[...]
        inner_mean = jnp.mean(scaled * normed, axis=1, keepdims=True)
        grad_x = inverse * (scaled - jnp.mean(scaled, axis=1, keepdims=True) - normed * inner_mean)
        grads_ref[rows] = keep_live(grad_x, lengths, span).astype(BF16)

    loop(0, steps // 4, last)
    in_stages[1]()
    out_stages[3]()
    loop(steps // 4, steps // 2, last)
    in_stages[2]()
    loop(steps // 2, steps, last)
    in_stages[3]()
    start_out(0, owners - 1, 2)
    sum_start(2)
    out_stages[4]()
    sum_middle(2)
    in_stages[4]()
    ln_ref[...] = sum_finish(2)
    in_stages[5]()
    out_stages[5]()

    def finish_copies(m):
        up_copy(m, 0, None, False).wait_send()
        sized(peer_of(m), lambda rows: up_copy(m, 1, rows, False).wait_send())
        for part in range(3):
            each_out(peer_of(m), m, part, True, lambda copy: copy.wait_recv())
            each_out(me, m, part, False, lambda copy: copy.wait_send())
        for n in range(3):
            b_copy(n, m, False).wait_send()

    loop(1, owners, finish_copies)

    def finish_sums(i):
        for n in range(3):
            a_copy(n, i, False).wait_send()

    loop(1, groups, finish_sums)


def finish_kernel(
    taps, per, per_out, piece, bounds,
    meta, grads_ref, arrived_ref, reduced_ref, reduced_out_ref, back_ref, ln_ref,
    out_ref, grad_frames_ref, win_ref, wout_ref, taps_ref, ln_out_ref, gain_ref, bias_ref,
    stage, flat, sems,
):
    me = lax.axis_index("bucket")
    owners, chunk, width = arrived_ref.shape
    own_rows = out_ref.shape[0]
    blocks = width // LANES
    share = win_ref.shape[0]
    wide = win_ref.shape[1] // LANES
    slots = sems.shape[0]
    span = grads_ref.shape[0] // slots

    def row_copy(i):
        source = pl.ds(pl.multiple_of(i * span, PACK), span)
        target = pl.ds(pl.multiple_of(meta[1, i] * span, PACK), span)
        return pltpu.make_async_copy(
            grads_ref.at[source], grad_frames_ref.at[target], sems.at[i]
        )

    def start(i, carry):
        row_copy(i).start()
        return carry

    lax.fori_loop(0, slots, start, 0)
    for b in range(owners):
        begin = meta[2, b]
        for c in range(blocks):
            stage[c, pl.ds(begin, bounds[b])] = arrived_ref[b, : bounds[b], lane(c)].astype(F32)
    for c in range(blocks):
        out_ref[:, lane(c)] = stage[c, :own_rows].astype(BF16)

    def section(source, count, s):
        q, r = s // count, s % count
        return source[q, r * share : (r + 1) * share].astype(F32)

    for c in range(blocks):
        wout_ref[:, lane(c)] = section(reduced_out_ref, per_out, c)
    for c in range(wide):
        win_ref[:, lane(c)] = section(reduced_ref, per, c)
    flat[...] = jnp.zeros_like(flat)
    for q in range(reduced_ref.shape[0]):
        flat[q * piece : (q + 1) * piece] = reduced_ref[
            q, per * share : per * share + piece
        ].astype(F32)
    taps_ref[...] = flat[...].T[:taps, :share]
    row = jnp.zeros((1, share), F32)
    for j in range(owners):
        c, n = j * share // LANES, j * share % LANES
        row = jnp.where(me == j, ln_ref[c : c + 1, n : n + share], row)
    ln_out_ref[...] = row
    bias_ref[...] = row_of(back_ref, 0, blocks)
    gain_ref[...] = row_of(back_ref, blocks, blocks)

    def wait(i, carry):
        row_copy(i).wait()
        return carry

    lax.fori_loop(0, slots, wait, 0)


def in_hbm(array):
    return pltpu.with_memory_space_constraint(array, pltpu.HBM)


def local(frames, lengths, owner_ids, upstream, ln_gain, w_in, w_dw, bn_gain, bn_bias, w_out):
    groups, owners = lax.axis_size("dp"), lax.axis_size("bucket")
    all_rows, width = frames.shape
    taps = w_dw.shape[1]
    slots = lengths.shape[1] // owners
    span = all_rows // slots
    pairs = slots // owners
    own_rows = upstream.shape[0]
    blocks = width // LANES
    wide = w_in.shape[1] // LANES
    total_frames = float(own_rows * owners * groups)
    in_vmem = pl.BlockSpec(memory_space=pltpu.VMEM)
    in_smem = pl.BlockSpec(memory_space=pltpu.SMEM)
    anywhere = pl.BlockSpec(memory_space=pl.ANY)
    group = pairs * max(1, 4 // pairs)
    size, fwd, inv, spec, corr = transform_tables(span, taps, group)
    chunk = pairs * span
    bounds = chunk_bounds(own_rows, pairs, span, owners)
    early = max(PACK, chunk // 3 // PACK * PACK)
    early_out = max(PACK, min(chunk * 5 // 12 // PACK * PACK, bounds[0] - PACK))
    late_out = max(early_out + PACK, chunk * 3 // 4 // PACK * PACK)
    share = width // owners
    per, per_out = -(-wide // groups), -(-blocks // groups)
    piece = share // groups
    sides = groups // 2
    rows_in = (per * share + -(-piece // PACK) * PACK, LANES)
    rows_out = (per_out * share, LANES)

    meta = pl.pallas_call(
        functools.partial(tables_kernel, slots),
        in_specs=[in_smem, in_smem],
        out_specs=in_smem,
        out_shape=jax.ShapeDtypeStruct((3, slots), jnp.int32),
        scratch_shapes=[pltpu.SMEM((owners,), jnp.int32)],
        compiler_params=pltpu.CompilerParams(vmem_limit_bytes=1 << 20),
        name="tables",
    )(in_hbm(lengths), in_hbm(owner_ids))

    operands = (
        upstream, w_dw.T, spec, frames.reshape(slots, span, width), w_in, ln_gain[None], fwd, inv,
        w_out, bn_gain[None], bn_bias[None], corr,
    )
    sums_shape = (2 * blocks, LANES)
    tall = pltpu.VMEM((all_rows, width), F32)
    short = pltpu.VMEM((all_rows, width), BF16)
    chunks = pltpu.VMEM((owners, chunk, width), BF16)

    def reduce_scratch(kind):
        return [
            pltpu.VMEM((owners, sides) + kind, BF16),
            pltpu.VMEM((owners, sides) + kind, BF16),
            pltpu.VMEM((sides, owners) + kind, BF16),
            pltpu.VMEM((owners,) + kind, BF16),
            pltpu.VMEM((owners // 2,) + kind, BF16),
            pltpu.VMEM((owners // 2,) + kind, BF16),
            pltpu.VMEM((owners // 2,) + kind, BF16),
            pltpu.VMEM(kind, BF16),
            pltpu.SemaphoreType.DMA((2, owners)),
            pltpu.SemaphoreType.DMA((2, sides * owners)),
            pltpu.SemaphoreType.DMA((2, owners // 2)),
            pltpu.SemaphoreType.DMA((2, owners // 2)),
            pltpu.SemaphoreType.DMA((2, groups)),
        ]

    grads, arrived, reduced, reduced_out, back, ln_total = pl.pallas_call(
        functools.partial(
            step_kernel,
            groups, owners, group, taps, size, early, early_out, late_out, bounds,
            total_frames,
        ),
        in_specs=[in_smem] + [anywhere] * 12,
        out_specs=[in_vmem] * 6,
        out_shape=[
            jax.ShapeDtypeStruct((all_rows, width), BF16),
            jax.ShapeDtypeStruct((owners, chunk, width), BF16),
            jax.ShapeDtypeStruct((groups,) + rows_in, BF16),
            jax.ShapeDtypeStruct((groups,) + rows_out, BF16),
            jax.ShapeDtypeStruct(sums_shape, F32),
            jax.ShapeDtypeStruct(sums_shape, F32),
        ],
        scratch_shapes=[pltpu.VMEM(operand.shape, operand.dtype) for operand in operands]
        + [
            pltpu.VMEM((blocks, own_rows + chunk, LANES), F32),
            chunks,
            chunks,
            chunks,
            tall,
            pltpu.VMEM((all_rows, LANES), F32),
            tall,
            tall,
            short,
            pltpu.VMEM((slots * size, width), F32),
            tall,
            tall,
            short,
            short,
            pltpu.VMEM((all_rows, w_in.shape[1]), BF16),
            pltpu.VMEM((taps + 1, width), F32),
            pltpu.VMEM((3 * size // 2, width), F32),
            pltpu.VMEM((2, SUB, width), F32),
            pltpu.VMEM((3 * size // 2, width), F32),
            pltpu.VMEM(sums_shape, F32),
            pltpu.VMEM((3,) + sums_shape, F32),
            pltpu.VMEM((3,) + sums_shape, F32),
            pltpu.VMEM((3, groups) + sums_shape, F32),
            pltpu.VMEM((3, owners) + sums_shape, F32),
            pltpu.VMEM((LANES, LANES), F32),
            pltpu.VMEM((owners, 2, sides) + rows_in, BF16),
            pltpu.VMEM((owners, 2, sides) + rows_out, BF16),
            pltpu.SemaphoreType.DMA((12,)),
            pltpu.SemaphoreType.DMA((2, owners)),
            pltpu.SemaphoreType.DMA((2, owners)),
            pltpu.SemaphoreType.DMA((3, owners)),
            pltpu.SemaphoreType.DMA((3, owners)),
            pltpu.SemaphoreType.DMA((3, groups)),
            pltpu.SemaphoreType.DMA((3, groups)),
            pltpu.SemaphoreType.DMA((3, owners)),
            pltpu.SemaphoreType.DMA((3, owners)),
        ]
        + reduce_scratch(rows_in)
        + reduce_scratch(rows_out),
        compiler_params=pltpu.CompilerParams(
            collective_id=0, has_side_effects=True, vmem_limit_bytes=STEP_VMEM
        ),
        cost_estimate=pl.CostEstimate(
            flops=10**10, bytes_accessed=4 * 10**7, transcendentals=0
        ),
        name="step",
    )(meta, *map(in_hbm, operands))

    row_shape = jax.ShapeDtypeStruct((1, width), F32)
    out_frames, grad_frames, grad_win, grad_wo, grad_taps, grad_ln, grad_gain, grad_bias = (
        pl.pallas_call(
            functools.partial(finish_kernel, taps, per, per_out, piece, bounds),
            in_specs=[in_smem] + [in_vmem] * 6,
            out_specs=[in_vmem, anywhere] + [in_vmem] * 6,
            out_shape=[
                jax.ShapeDtypeStruct((own_rows, width), BF16),
                jax.ShapeDtypeStruct((all_rows, width), BF16),
                jax.ShapeDtypeStruct((share, w_in.shape[1]), F32),
                jax.ShapeDtypeStruct((share, width), F32),
                jax.ShapeDtypeStruct((taps, share), F32),
                jax.ShapeDtypeStruct((1, share), F32),
                row_shape,
                row_shape,
            ],
            scratch_shapes=[
                pltpu.VMEM((blocks, own_rows + chunk, LANES), F32),
                pltpu.VMEM((LANES, LANES), F32),
                pltpu.SemaphoreType.DMA((slots,)),
            ],
            compiler_params=pltpu.CompilerParams(vmem_limit_bytes=8 << 20),
            name="finish",
        )(meta, grads, arrived, reduced, reduced_out, back, ln_total)
    )
    return (
        out_frames,
        grad_frames,
        grad_win,
        grad_wo,
        grad_taps.T,
        grad_ln[0],
        grad_gain[0],
        grad_bias[0],
    )


def solution(mesh):
    placed = (
        P(("dp", "bucket"), None),
        P("dp", None),
        P("dp", None),
        P(("dp", "bucket"), None),
        P(),
        P(),
        P(),
        P(),
        P(),
        P(),
    )
    return jax.shard_map(
        local,
        mesh=mesh,
        in_specs=placed,
        out_specs=(
            P(("dp", "bucket"), None),
            P(("dp", "bucket"), None),
            P("bucket", None),
            P("bucket", None),
            P("bucket", None),
            P("bucket"),
            P(),
            P(),
        ),
        check_vma=False,
    )
```

time: 116 us -> 98.6 us (0.85)
  Pallas kernels: 108 us -> 97.8 us
  local copies, waits for them, and re-layouts: 6.59 us -> 0 us
    pallas_call x1, Pallas kernels: 102 us -> 92.3 us  [local(): pl.pallas_call(functools.partial(step_kernel, groups, owners, group, taps...]
    unnamed x12 -> x0, local copies, waits for them, and re-layouts: 5.11 us -> none
    pad x1 -> x0, local copies, waits for them, and re-layouts: 1.48 us -> none  [local(): jnp.pad(w_dw.T, ((0, 1), (0, 0)))]
where the time goes in v2:
time: 98.6 us; the launch traced here: 98.4 us
  Pallas kernels  97.8 us (99%)
    pallas_call x1, Pallas kernels, local(): pl.pallas_call(functools.partial(step_kernel, groups, owners, group, taps...  92.3 us
    pallas_call x1, Pallas kernels, local(): pl.pallas_call(functools.partial(finish_kernel, taps, per, per_out, piece...  3.15 us
    pallas_call x1, Pallas kernels, local(): pl.pallas_call(functools.partial(tables_kernel, slots), in_specs=[in_smem...  2.37 us

profile of v2, /device:TPU:0, one launch (start us, length us, event | category | flops | bytes accessed | tf_op | source)
XLA Modules:
  0.0 98.4 jit_solution(5178661884900894813)
XLA Ops:
  0.6 2.4 %tables.1.meta = s32[3,32]{1,0:T(4,128)S(1)} custom-call(s32[1,256]{1,0:T(1,128)} %lens_ref.1, s32[1,256]{1,0:T(1,128)} %owners_ref.1), custom_call_target="tpu_custom_call" | custom-call | tf_op jit(solution)/shard_map/tables/pallas_call | solution.py:796
  3.0 92.3 %step.1 = (bf16[1536,512]{1,0:T(8,128)(2,1)S(1)}, bf16[8,192,512]{2,1,0:T(8,128)(2,1)S(1)}, bf16[4,144,128]{2,1,0:T(8,128)(2,1)S(1)}, bf16[4,64,128]{2,1,0:T(8,1...) custom-call(s32[3,32]{1,0:T(4,128)S(1)} %tables.1.meta, bf16[768,512]{1,0:T(8,128)(2,1)} %refs_0_.1, ...), custom_call_target="tpu_custom_call" | custom-call | flops 10000000000 | bytes 40000000 | tf_op jit(solution)/shard_map/step/pallas_call | solution.py:832
  95.3 3.1 %finish.1 = (bf16[768,512]{1,0:T(8,128)(2,1)}, bf16[1536,512]{1,0:T(8,128)(2,1)}, f32[64,1024]{1,0:T(8,128)}, f32[64,512]{1,0:T(8,128)}, f32[31,64]{1,0:T(8,128)...) custom-call(s32[3,32]{1,0:T(4,128)S(1)} %tables.1.meta, ...), custom_call_target="tpu_custom_call" | custom-call | tf_op jit(solution)/shard_map/finish/pallas_call | solution.py:900

commit v3 on v2

--- a/solution.py
+++ b/solution.py
@@ -150,20 +150,23 @@
             device_id_type=MESH,
         )
 
-    def bucket_of(i):
-        return lax.rem(me + 1 + i, owners)
-
-    def swap(i):
-        bucket = bucket_of(i)
-        return remote(src.at[bucket, 1 - core], first.at[bucket], core_sems, i, i, (partner, me))
-
-    def to_side(i, n, arriving):
-        bucket = bucket_of(i)
-        other = lax.rem(side + n, sides)
+    wave = owners // 2
+
+    def wave_of(h):
+        return pl.ds(h * wave, wave)
+
+    def swap(h):
+        return remote(
+            src.at[wave_of(h), 1 - core], first.at[wave_of(h)], core_sems, h, h, (partner, me)
+        )
+
+    def to_side(h, n, arriving):
+        other = lax.rem(side + (sides - n if arriving else n), sides)
         slot = other if arriving else side
+        target = lax.rem(side + n, sides)
         return remote(
-            first_sum.at[bucket, other], second.at[slot, bucket], pair_sems,
-            n * owners + i, slot * owners + i, (other * 2 + core, me),
+            first_sum.at[target, wave_of(h)], second.at[slot, wave_of(h)], pair_sems,
+            h * sides + n, h * sides + n, (target * 2 + core, me),
         )
 
     near = lax.rem(me, 2)
@@ -173,9 +176,8 @@
     def pair_of(i):
         return lax.rem(me // 2 + 1 + i, pairs)
 
-    def to_mate(i):
-        pair = pair_of(i)
-        return remote(second_sum.at[pair * 2 + 1 - near], twin.at[pair], twin_sems, i, i, (dp, mate))
+    def to_mate():
+        return remote(second_sum.at[:, 1 - near], twin, twin_sems, 0, 0, (dp, mate))
 
     def to_owner(i, arriving):
         pair = lax.rem(me // 2 + i, pairs)
@@ -197,43 +199,48 @@
 
         lax.fori_loop(low, high, step, 0)
 
+    def stage_swap():
+        for h in range(2):
+            swap(h).start()
+
     def add_first(i):
-        bucket = bucket_of(i)
-        swap(i).wait_recv()
-        total = src[bucket, core].astype(F32) + first[bucket].astype(F32)
-        first_sum[bucket] = total.astype(BF16)
-        for n in range(1, sides):
-            to_side(i, n, False).start()
+        total = src[i, core].astype(F32) + first[i].astype(F32)
+        for n in range(sides):
+            first_sum[n, i] = total[n].astype(BF16)
+
+    def stage_side():
+        for h in range(2):
+            swap(h).wait_recv()
+            loop(h * wave, (h + 1) * wave, add_first)
+            for n in range(1, sides):
+                to_side(h, n, False).start()
 
     def add_second(i):
-        bucket = bucket_of(i)
-        total = first_sum[bucket, side].astype(F32)
-        for n in range(1, sides):
-            to_side(i, n, True).wait_recv()
-            total = total + second[lax.rem(side + n, sides), bucket].astype(F32)
-        second_sum[bucket] = total.astype(BF16)
+        for half in range(2):
+            bucket = i * 2 + half
+            total = first_sum[side, bucket].astype(F32)
+            for n in range(1, sides):
+                total = total + second[lax.rem(side + n, sides), bucket].astype(F32)
+            second_sum[i, half] = total.astype(BF16)
+
+    def stage_mate():
+        for h in range(2):
+            for n in range(1, sides):
+                to_side(h, n, True).wait_recv()
+        loop(0, pairs, add_second)
+        to_mate().start()
 
     def add_twin(i):
         pair = pair_of(i)
-        to_mate(i).wait_recv()
-        total = second_sum[pair * 2 + near].astype(F32) + twin[pair].astype(F32)
+        total = second_sum[pair, near].astype(F32) + twin[pair].astype(F32)
         twin_sum[pair] = total.astype(BF16)
 
     def twin_and_send(i):
         add_twin(i)
         to_owner(i + 1, False).start()
 
-    def stage_swap():
-        loop(0, owners, lambda i: swap(i).start())
-
-    def stage_side():
-        loop(0, owners, add_first)
-
-    def stage_mate():
-        loop(0, owners, add_second)
-        loop(0, pairs, lambda i: to_mate(i).start())
-
     def stage_owner():
+        to_mate().wait_recv()
         loop(0, pairs - 1, twin_and_send)
         add_twin(pairs - 1)
         third[me // 2] = twin_sum[me // 2]
@@ -250,13 +257,11 @@
     def stage_end():
         loop(1, groups, lambda i: to_group(i, True).wait_recv())
 
-        def first_sent(i):
-            swap(i).wait_send()
+        for h in range(2):
+            swap(h).wait_send()
             for n in range(1, sides):
-                to_side(i, n, False).wait_send()
-
-        loop(0, owners, first_sent)
-        loop(0, pairs, lambda i: to_mate(i).wait_send())
+                to_side(h, n, False).wait_send()
+        to_mate().wait_send()
         loop(1, pairs, lambda i: to_owner(i, False).wait_send())
         loop(1, groups, lambda i: to_group(i, False).wait_send())
 
@@ -264,7 +269,7 @@
 
 
 def step_kernel(
-    groups, owners, group, taps, size, early, early_out, late_out, bounds, total_frames,
+    groups, owners, group, taps, size, early, early_out, bounds, total_frames,
     meta, *refs,
 ):
     sources, refs = refs[:12], refs[12:]
@@ -357,7 +362,7 @@
             device_id_type=MESH,
         )
 
-    cuts = (0, early_out, late_out, chunk)
+    cuts = (0, early_out, chunk)
 
     def out_copy(m, part, rows, arriving):
         peer = peer_of(m)
@@ -402,7 +407,7 @@
         return pltpu.make_async_remote_copy(
             src_ref=parts.at[n],
             dst_ref=slots_a.at[n, slot],
-            send_sem=a_send.at[n, i],
+            send_sem=a_send.at[i],
             recv_sem=a_recv.at[n, i],
             device_id=(other, me),
             device_id_type=MESH,
@@ -414,7 +419,7 @@
         return pltpu.make_async_remote_copy(
             src_ref=mids.at[n],
             dst_ref=slots_b.at[n, slot],
-            send_sem=b_send.at[n, m],
+            send_sem=b_send.at[m],
             recv_sem=b_recv.at[n, m],
             device_id=(dp, peer),
             device_id_type=MESH,
@@ -436,6 +441,8 @@
 
     def sum_finish(n):
         loop(1, owners, lambda m: b_copy(n, m, True).wait_recv())
+        loop(1, groups, lambda i: a_copy(n, i, False).wait_send())
+        loop(1, owners, lambda m: b_copy(n, m, False).wait_send())
         return lax.fori_loop(1, owners, lambda i, t: t + slots_b[n, i], slots_b[n, 0])
 
     loads[1].wait()
@@ -667,14 +674,12 @@
     loop(0, steps // 4, last)
     in_stages[1]()
     out_stages[3]()
-    loop(steps // 4, steps // 2, last)
+    loop(steps // 4, steps, last)
+    sum_start(2)
     in_stages[2]()
-    loop(steps // 2, steps, last)
+    sum_middle(2)
     in_stages[3]()
-    start_out(0, owners - 1, 2)
-    sum_start(2)
     out_stages[4]()
-    sum_middle(2)
     in_stages[4]()
     ln_ref[...] = sum_finish(2)
     in_stages[5]()
@@ -683,19 +688,10 @@
     def finish_copies(m):
         up_copy(m, 0, None, False).wait_send()
         sized(peer_of(m), lambda rows: up_copy(m, 1, rows, False).wait_send())
-        for part in range(3):
+        for part in range(2):
             each_out(peer_of(m), m, part, True, lambda copy: copy.wait_recv())
             each_out(me, m, part, False, lambda copy: copy.wait_send())
-        for n in range(3):
-            b_copy(n, m, False).wait_send()
-
     loop(1, owners, finish_copies)
-
-    def finish_sums(i):
-        for n in range(3):
-            a_copy(n, i, False).wait_send()
-
-    loop(1, groups, finish_sums)
 
 
 def finish_kernel(
@@ -783,9 +779,8 @@
     size, fwd, inv, spec, corr = transform_tables(span, taps, group)
     chunk = pairs * span
     bounds = chunk_bounds(own_rows, pairs, span, owners)
-    early = max(PACK, chunk // 3 // PACK * PACK)
+    early = max(PACK, min(chunk // 2 // PACK * PACK, bounds[0] - PACK))
     early_out = max(PACK, min(chunk * 5 // 12 // PACK * PACK, bounds[0] - PACK))
-    late_out = max(early_out + PACK, chunk * 3 // 4 // PACK * PACK)
     share = width // owners
     per, per_out = -(-wide // groups), -(-blocks // groups)
     piece = share // groups
@@ -815,16 +810,16 @@
     def reduce_scratch(kind):
         return [
             pltpu.VMEM((owners, sides) + kind, BF16),
-            pltpu.VMEM((owners, sides) + kind, BF16),
             pltpu.VMEM((sides, owners) + kind, BF16),
-            pltpu.VMEM((owners,) + kind, BF16),
+            pltpu.VMEM((sides, owners) + kind, BF16),
+            pltpu.VMEM((owners // 2, 2) + kind, BF16),
             pltpu.VMEM((owners // 2,) + kind, BF16),
             pltpu.VMEM((owners // 2,) + kind, BF16),
             pltpu.VMEM((owners // 2,) + kind, BF16),
             pltpu.VMEM(kind, BF16),
-            pltpu.SemaphoreType.DMA((2, owners)),
-            pltpu.SemaphoreType.DMA((2, sides * owners)),
-            pltpu.SemaphoreType.DMA((2, owners // 2)),
+            pltpu.SemaphoreType.DMA((2, 2)),
+            pltpu.SemaphoreType.DMA((2, 2 * sides)),
+            pltpu.SemaphoreType.DMA((2, 1)),
             pltpu.SemaphoreType.DMA((2, owners // 2)),
             pltpu.SemaphoreType.DMA((2, groups)),
         ]
@@ -832,7 +827,7 @@
     grads, arrived, reduced, reduced_out, back, ln_total = pl.pallas_call(
         functools.partial(
             step_kernel,
-            groups, owners, group, taps, size, early, early_out, late_out, bounds,
+            groups, owners, group, taps, size, early, early_out, bounds,
             total_frames,
         ),
         in_specs=[in_smem] + [anywhere] * 12,
@@ -877,11 +872,11 @@
             pltpu.SemaphoreType.DMA((12,)),
             pltpu.SemaphoreType.DMA((2, owners)),
             pltpu.SemaphoreType.DMA((2, owners)),
-            pltpu.SemaphoreType.DMA((3, owners)),
-            pltpu.SemaphoreType.DMA((3, owners)),
+            pltpu.SemaphoreType.DMA((2, owners)),
+            pltpu.SemaphoreType.DMA((2, owners)),
+            pltpu.SemaphoreType.DMA((groups,)),
             pltpu.SemaphoreType.DMA((3, groups)),
-            pltpu.SemaphoreType.DMA((3, groups)),
-            pltpu.SemaphoreType.DMA((3, owners)),
+            pltpu.SemaphoreType.DMA((owners,)),
             pltpu.SemaphoreType.DMA((3, owners)),
         ]
         + reduce_scratch(rows_in)

time: 98.6 us -> 92.2 us (0.935)
  Pallas kernels: 97.8 us -> 91.4 us
    pallas_call x1, Pallas kernels: 92.3 us -> 85.9 us  [local(): pl.pallas_call(functools.partial(step_kernel, groups, owners, group, taps...]
where the time goes in v3:
time: 92.2 us; the launch traced here: 92.1 us
  Pallas kernels  91.4 us (99%)
    pallas_call x1, Pallas kernels, local(): pl.pallas_call(functools.partial(step_kernel, groups, owners, group, taps...  85.9 us
    pallas_call x1, Pallas kernels, local(): pl.pallas_call(functools.partial(finish_kernel, taps, per, per_out, piece...  3.15 us
    pallas_call x1, Pallas kernels, local(): pl.pallas_call(functools.partial(tables_kernel, slots), in_specs=[in_smem...  2.37 us

profile of v3, /device:TPU:0, one launch (start us, length us, event | category | flops | bytes accessed | tf_op | source)
XLA Modules:
  0.0 92.1 jit_solution(12593151262042194301)
XLA Ops:
  0.6 2.4 %tables.1.meta = s32[3,32]{1,0:T(4,128)S(1)} custom-call(s32[1,256]{1,0:T(1,128)} %lens_ref.1, s32[1,256]{1,0:T(1,128)} %owners_ref.1), custom_call_target="tpu_custom_call" | custom-call | tf_op jit(solution)/shard_map/tables/pallas_call | solution.py:791
  3.0 85.9 %step.1 = (bf16[1536,512]{1,0:T(8,128)(2,1)S(1)}, bf16[8,192,512]{2,1,0:T(8,128)(2,1)S(1)}, bf16[4,144,128]{2,1,0:T(8,128)(2,1)S(1)}, bf16[4,64,128]{2,1,0:T(8,1...) custom-call(s32[3,32]{1,0:T(4,128)S(1)} %tables.1.meta, bf16[768,512]{1,0:T(8,128)(2,1)} %refs_0_.1, ...), custom_call_target="tpu_custom_call" | custom-call | flops 10000000000 | bytes 40000000 | tf_op jit(solution)/shard_map/step/pallas_call | solution.py:827
  88.9 3.1 %finish.1 = (bf16[768,512]{1,0:T(8,128)(2,1)}, bf16[1536,512]{1,0:T(8,128)(2,1)}, f32[64,1024]{1,0:T(8,128)}, f32[64,512]{1,0:T(8,128)}, f32[31,64]{1,0:T(8,128)...) custom-call(s32[3,32]{1,0:T(4,128)S(1)} %tables.1.meta, ...), custom_call_target="tpu_custom_call" | custom-call | tf_op jit(solution)/shard_map/finish/pallas_call | solution.py:895

commit v4 on v3

--- a/solution.py
+++ b/solution.py
@@ -199,9 +199,8 @@
 
         lax.fori_loop(low, high, step, 0)
 
-    def stage_swap():
-        for h in range(2):
-            swap(h).start()
+    def stage_swap(h):
+        swap(h).start()
 
     def add_first(i):
         total = src[i, core].astype(F32) + first[i].astype(F32)
@@ -597,7 +596,8 @@
             j = c * (LANES // share) + n
             for s in range(blocks):
                 put(packed_out, per_out, j, s, grad[n * share : (n + 1) * share, lane(s)])
-    out_stages[0]()
+        if c % (blocks // 2) == blocks // 2 - 1:
+            out_stages[0](c // (blocks // 2))
     back_ref[...] = sum_finish(1)
 
     @pl.when(me < far)
@@ -639,9 +639,16 @@
         ga_s[rows, :width] = left.astype(BF16)
         ga_s[rows, width:] = (left * linear_s[rows] * (1.0 - gate)).astype(BF16)
 
-    loop(0, steps // 2, backward)
+    def twice(body):
+        def both(i):
+            body(2 * i)
+            body(2 * i + 1)
+
+        return both
+
+    loop(0, steps // 4, twice(backward))
     out_stages[1]()
-    loop(steps // 2, steps, backward)
+    loop(steps // 4, steps // 2, twice(backward))
     out_stages[2]()
     grad_taps = matmul_exact(corr_ref[...], xacc[...])
     flat[...] = jnp.zeros_like(flat)
@@ -657,7 +664,8 @@
                 packed[j, q // sides, q % sides, per * share : per * share + piece] = turned[
                     n * share + q * piece : n * share + (q + 1) * piece
                 ]
-    in_stages[0]()
+        if c % (blocks // 2) == blocks // 2 - 1:
+            in_stages[0](c // (blocks // 2))
     acc[...] = jnp.zeros_like(acc)
 
     def last(i):
@@ -697,8 +705,9 @@
 def finish_kernel(
     taps, per, per_out, piece, bounds,
     meta, grads_ref, arrived_ref, reduced_ref, reduced_out_ref, back_ref, ln_ref,
-    out_ref, grad_frames_ref, win_ref, wout_ref, taps_ref, ln_out_ref, gain_ref, bias_ref,
-    stage, flat, sems,
+    out_hbm, grad_frames_ref, win_hbm, wout_hbm, taps_hbm, ln_hbm, gain_hbm, bias_hbm,
+    out_ref, win_ref, wout_ref, taps_ref, ln_out_ref, gain_ref, bias_ref,
+    stage, flat, sems, ends,
 ):
     me = lax.axis_index("bucket")
     owners, chunk, width = arrived_ref.shape
@@ -708,6 +717,11 @@
     wide = win_ref.shape[1] // LANES
     slots = sems.shape[0]
     span = grads_ref.shape[0] // slots
+    copies = []
+
+    def send(source, target):
+        copies.append(pltpu.make_async_copy(source, target, ends.at[len(copies)]))
+        copies[-1].start()
 
     def row_copy(i):
         source = pl.ds(pl.multiple_of(i * span, PACK), span)
@@ -727,34 +741,43 @@
             stage[c, pl.ds(begin, bounds[b])] = arrived_ref[b, : bounds[b], lane(c)].astype(F32)
     for c in range(blocks):
         out_ref[:, lane(c)] = stage[c, :own_rows].astype(BF16)
+    send(out_ref, out_hbm)
 
     def section(source, count, s):
         q, r = s // count, s % count
         return source[q, r * share : (r + 1) * share].astype(F32)
 
+    for c in range(wide):
+        win_ref[:, lane(c)] = section(reduced_ref, per, c)
+    send(win_ref, win_hbm)
     for c in range(blocks):
         wout_ref[:, lane(c)] = section(reduced_out_ref, per_out, c)
-    for c in range(wide):
-        win_ref[:, lane(c)] = section(reduced_ref, per, c)
+    send(wout_ref, wout_hbm)
+    row = jnp.zeros((1, share), F32)
+    for j in range(owners):
+        c, n = j * share // LANES, j * share % LANES
+        row = jnp.where(me == j, ln_ref[c : c + 1, n : n + share], row)
+    ln_out_ref[...] = row
+    send(ln_out_ref, ln_hbm)
+    bias_ref[...] = row_of(back_ref, 0, blocks)
+    send(bias_ref, bias_hbm)
+    gain_ref[...] = row_of(back_ref, blocks, blocks)
+    send(gain_ref, gain_hbm)
     flat[...] = jnp.zeros_like(flat)
     for q in range(reduced_ref.shape[0]):
         flat[q * piece : (q + 1) * piece] = reduced_ref[
             q, per * share : per * share + piece
         ].astype(F32)
     taps_ref[...] = flat[...].T[:taps, :share]
-    row = jnp.zeros((1, share), F32)
-    for j in range(owners):
-        c, n = j * share // LANES, j * share % LANES
-        row = jnp.where(me == j, ln_ref[c : c + 1, n : n + share], row)
-    ln_out_ref[...] = row
-    bias_ref[...] = row_of(back_ref, 0, blocks)
-    gain_ref[...] = row_of(back_ref, blocks, blocks)
+    send(taps_ref, taps_hbm)
 
     def wait(i, carry):
         row_copy(i).wait()
         return carry
 
     lax.fori_loop(0, slots, wait, 0)
+    for copy in copies:
+        copy.wait()
 
 
 def in_hbm(array):
@@ -890,26 +913,28 @@
         name="step",
     )(meta, *map(in_hbm, operands))
 
-    row_shape = jax.ShapeDtypeStruct((1, width), F32)
+    results = [jax.ShapeDtypeStruct((own_rows, width), BF16)] + [
+        jax.ShapeDtypeStruct(shape, F32)
+        for shape in (
+            (share, w_in.shape[1]), (share, width), (taps, share), (1, share), (1, width), (1, width)
+        )
+    ]
     out_frames, grad_frames, grad_win, grad_wo, grad_taps, grad_ln, grad_gain, grad_bias = (
         pl.pallas_call(
             functools.partial(finish_kernel, taps, per, per_out, piece, bounds),
             in_specs=[in_smem] + [in_vmem] * 6,
-            out_specs=[in_vmem, anywhere] + [in_vmem] * 6,
+            out_specs=[anywhere] * 8,
             out_shape=[
-                jax.ShapeDtypeStruct((own_rows, width), BF16),
+                results[0],
                 jax.ShapeDtypeStruct((all_rows, width), BF16),
-                jax.ShapeDtypeStruct((share, w_in.shape[1]), F32),
-                jax.ShapeDtypeStruct((share, width), F32),
-                jax.ShapeDtypeStruct((taps, share), F32),
-                jax.ShapeDtypeStruct((1, share), F32),
-                row_shape,
-                row_shape,
+                *results[1:],
             ],
-            scratch_shapes=[
+            scratch_shapes=[pltpu.VMEM(result.shape, result.dtype) for result in results]
+            + [
                 pltpu.VMEM((blocks, own_rows + chunk, LANES), F32),
                 pltpu.VMEM((LANES, LANES), F32),
                 pltpu.SemaphoreType.DMA((slots,)),
+                pltpu.SemaphoreType.DMA((len(results),)),
             ],
             compiler_params=pltpu.CompilerParams(vmem_limit_bytes=8 << 20),
             name="finish",

time: 92.2 us -> 91 us (0.987)
  Pallas kernels: 91.4 us -> 89.5 us
    pallas_call x1, Pallas kernels: 85.9 us -> 84.2 us  [local(): pl.pallas_call(functools.partial(step_kernel, groups, owners, group, taps...]
where the time goes in v4:
time: 91 us; the launch traced here: 90.1 us
  Pallas kernels  89.5 us (98%)
    pallas_call x1, Pallas kernels, local(): pl.pallas_call(functools.partial(step_kernel, groups, owners, group, taps...  84.2 us
    pallas_call x1, Pallas kernels, local(): pl.pallas_call(functools.partial(finish_kernel, taps, per, per_out, piece...  2.93 us
    pallas_call x1, Pallas kernels, local(): pl.pallas_call(functools.partial(tables_kernel, slots), in_specs=[in_smem...  2.37 us

profile of v4, /device:TPU:0, one launch (start us, length us, event | category | flops | bytes accessed | tf_op | source)
XLA Modules:
  0.0 90.1 jit_solution(1809586965172072811)
XLA Ops:
  0.6 2.4 %tables.1.meta = s32[3,32]{1,0:T(4,128)S(1)} custom-call(s32[1,256]{1,0:T(1,128)} %lens_ref.1, s32[1,256]{1,0:T(1,128)} %owners_ref.1), custom_call_target="tpu_custom_call" | custom-call | tf_op jit(solution)/shard_map/tables/pallas_call | solution.py:814
  3.0 84.2 %step.1 = (bf16[1536,512]{1,0:T(8,128)(2,1)S(1)}, bf16[8,192,512]{2,1,0:T(8,128)(2,1)S(1)}, bf16[4,144,128]{2,1,0:T(8,128)(2,1)S(1)}, bf16[4,64,128]{2,1,0:T(8,1...) custom-call(s32[3,32]{1,0:T(4,128)S(1)} %tables.1.meta, bf16[768,512]{1,0:T(8,128)(2,1)} %refs_0_.1, ...), custom_call_target="tpu_custom_call" | custom-call | flops 10000000000 | bytes 40000000 | tf_op jit(solution)/shard_map/step/pallas_call | solution.py:850
  87.2 2.9 %finish.1 = (bf16[768,512]{1,0:T(8,128)(2,1)}, bf16[1536,512]{1,0:T(8,128)(2,1)}, f32[64,1024]{1,0:T(8,128)}, f32[64,512]{1,0:T(8,128)}, f32[31,64]{1,0:T(8,128)...) custom-call(s32[3,32]{1,0:T(4,128)S(1)} %tables.1.meta, ...), custom_call_target="tpu_custom_call" | custom-call | tf_op jit(solution)/shard_map/finish/pallas_call | solution.py:923

commit v5 on v4

--- a/solution.py
+++ b/solution.py
@@ -331,13 +331,12 @@
         stage[c, :own_rows] = up[:, lane(c)].astype(F32)
         stage[c, own_rows:] = jnp.zeros((chunk, LANES), F32)
 
-    def lay_out(b):
-        start = meta[2, b]
+    def lay_out(b, low, high):
+        start = meta[2, b] + low
         for c in range(blocks):
-            outgoing[b, :, lane(c)] = stage[c, pl.ds(start, chunk)].astype(BF16)
-
-    loop(0, owners, lay_out)
-    arrive[me] = outgoing[me]
+            outgoing[b, low:high, lane(c)] = stage[c, pl.ds(start, high - low)].astype(BF16)
+
+    loop(0, owners, lambda b: lay_out(b, 0, early))
 
     def sized(index, body):
         for rows in sorted(set(bounds)):
@@ -452,6 +451,8 @@
     acc[...] = jnp.zeros_like(acc)
     pl.semaphore_wait(barrier, groups + owners - 2)
     start_up(0)
+    loop(0, owners, lambda b: lay_out(b, early, chunk))
+    arrive[me] = outgoing[me]
     for load in loads[3:8]:
         load.wait()
 

time: 91 us -> 90.9 us (level)
  no operation moved by 1% of the time
where the time goes in v5:
time: 90.9 us; the launch traced here: 90 us
  Pallas kernels  89.4 us (98%)
    pallas_call x1, Pallas kernels, local(): pl.pallas_call(functools.partial(step_kernel, groups, owners, group, taps...  84.1 us
    pallas_call x1, Pallas kernels, local(): pl.pallas_call(functools.partial(finish_kernel, taps, per, per_out, piece...  2.93 us
    pallas_call x1, Pallas kernels, local(): pl.pallas_call(functools.partial(tables_kernel, slots), in_specs=[in_smem...  2.37 us

profile of v5, /device:TPU:0, one launch (start us, length us, event | category | flops | bytes accessed | tf_op | source)
XLA Modules:
  0.0 90.0 jit_solution(2241745712027585816)
XLA Ops:
  0.6 2.4 %tables.1.meta = s32[3,32]{1,0:T(4,128)S(1)} custom-call(s32[1,256]{1,0:T(1,128)} %lens_ref.1, s32[1,256]{1,0:T(1,128)} %owners_ref.1), custom_call_target="tpu_custom_call" | custom-call | tf_op jit(solution)/shard_map/tables/pallas_call | solution.py:815
  3.0 84.1 %step.1 = (bf16[1536,512]{1,0:T(8,128)(2,1)S(1)}, bf16[8,192,512]{2,1,0:T(8,128)(2,1)S(1)}, bf16[4,144,128]{2,1,0:T(8,128)(2,1)S(1)}, bf16[4,64,128]{2,1,0:T(8,1...) custom-call(s32[3,32]{1,0:T(4,128)S(1)} %tables.1.meta, bf16[768,512]{1,0:T(8,128)(2,1)} %refs_0_.1, ...), custom_call_target="tpu_custom_call" | custom-call | flops 10000000000 | bytes 40000000 | tf_op jit(solution)/shard_map/step/pallas_call | solution.py:851
  87.1 2.9 %finish.1 = (bf16[768,512]{1,0:T(8,128)(2,1)}, bf16[1536,512]{1,0:T(8,128)(2,1)}, f32[64,1024]{1,0:T(8,128)}, f32[64,512]{1,0:T(8,128)}, f32[31,64]{1,0:T(8,128)...) custom-call(s32[3,32]{1,0:T(4,128)S(1)} %tables.1.meta, ...), custom_call_target="tpu_custom_call" | custom-call | tf_op jit(solution)/shard_map/finish/pallas_call | solution.py:924
